TPU v7x, 32 devices: a whole 2x2x4 slice. The times are simulated.
32 devices in a mesh: band: 4 (over x, core), slab: 8 (over z, y).
Axes of the slice: x: 2, y: 2, z: 4, core: 2. Of those that a mesh axis runs over, the one named last changes fastest.
Arguments:
- resident: float32 [8, 128, 128, 128], P('band', 'slab'), may hold values from -5 to 5
- blocks: float32 [16, 128, 128, 128], P('band', 'slab'), may hold values from -5 to 5
- occupation: float32 [16], replicated, may hold values from 0.25 to 1
Outputs:
- exchange_term: float32 [8, 128, 128, 128], P('band', 'slab')
All inputs are finite; a program needn't handle non-finite values.
Results may differ from a plain program's by a relative error of at most 0.0001.
Values sent between devices are 32-bit elements; how exact they have to be, the bound alone decides.
No kernel may reach another device: no remote copies, remote signals or barrier semaphores. Data moves between devices by JAX's collectives and lax.ppermute only.
A program may use at most 192 MiB of HBM per device.

v0:
```python
import functools
import math

import jax
import jax.numpy as jnp
from jax import lax
from jax.experimental import pallas as pl
from jax.experimental.pallas import tpu as pltpu
from jax.sharding import PartitionSpec as P


KAPPA_SQ = 0.01
F32, BF16 = (jnp.float32, jnp.bfloat16)


def dft_tables(grid_len):
    indices = jnp.arange(grid_len, dtype=jnp.int32)
    product = indices[:, None] * indices[None, :] % grid_len
    angles = product.astype(jnp.float32) * (2.0 * math.pi / grid_len)
    return (jnp.cos(angles), jnp.sin(angles))


def transform(real_part, imag_part, form, cos_t, sin_t, sign_val):

    def apply(values, table):
        return jnp.einsum(
            form, values, table, precision=lax.Precision.HIGHEST, preferred_element_type=jnp.float32
        )

    real_cos = apply(real_part, cos_t)
    real_sin = apply(real_part, sin_t)
    imag_cos = apply(imag_part, cos_t)
    imag_sin = apply(imag_part, sin_t)
    return (real_cos - sign_val * imag_sin, imag_cos + sign_val * real_sin)


def wave_of(indices, grid_len):
    signed = jnp.where(indices > (grid_len - 1) // 2, indices - grid_len, indices)
    return signed.astype(jnp.float32) * (2.0 * math.pi / grid_len)


def coulomb(wave_z, wave_y, wave_x):
    squared = wave_z[:, None, None] ** 2 + wave_y[None, :, None] ** 2 + wave_x[None, None, :] ** 2
    return 4.0 * math.pi / (squared + KAPPA_SQ)


def sliced_grids(resident, blocks, occupation):
    orb_count, plane_count, grid_len, _ = resident.shape
    local_src = blocks.shape[0]
    group_count = lax.axis_size("band")
    src_count = local_src * group_count
    cos_t, sin_t = dft_tables(grid_len)
    along_x = "fzyx,xk->fzyk"
    along_y = "fzyx,yk->fzkx"
    along_z = "fzyx,zk->fkyx"
    source = lax.all_gather(blocks, "band", axis=0, tiled=True)
    count_pairs = source.shape[0] // 2
    even_src = source[0::2]
    odd_src = source[1::2]
    real_part = (resident[:, None] * even_src[None]).reshape(
        orb_count * count_pairs, plane_count, grid_len, grid_len
    )
    imag_part = (resident[:, None] * odd_src[None]).reshape(
        orb_count * count_pairs, plane_count, grid_len, grid_len
    )
    real_part, imag_part = transform(real_part, imag_part, along_x, cos_t, sin_t, -1.0)
    real_part, imag_part = transform(real_part, imag_part, along_y, cos_t, sin_t, -1.0)
    shaped = (orb_count, count_pairs, plane_count, grid_len, grid_len)
    real_part, imag_part = (real_part.reshape(shaped), imag_part.reshape(shaped))
    field_count = orb_count * (src_count // 2)
    flat = (field_count, plane_count, grid_len, grid_len)
    real_part = real_part.reshape(flat)
    imag_part = imag_part.reshape(flat)
    all_waves = wave_of(jnp.arange(grid_len, dtype=jnp.int32), grid_len)
    position = lax.axis_index("slab")
    col_real = lax.all_to_all(real_part, "slab", split_axis=2, concat_axis=1, tiled=True)
    col_imag = lax.all_to_all(imag_part, "slab", split_axis=2, concat_axis=1, tiled=True)
    width_y = col_real.shape[2]
    local_waves = wave_of(position * width_y + jnp.arange(width_y, dtype=jnp.int32), grid_len)
    kernel = coulomb(all_waves, local_waves, all_waves)
    col_real, col_imag = transform(col_real, col_imag, along_z, cos_t, sin_t, -1.0)
    col_real = col_real * kernel[None]
    col_imag = col_imag * kernel[None]
    col_real, col_imag = transform(col_real, col_imag, along_z, cos_t, sin_t, 1.0)
    real_part = lax.all_to_all(col_real, "slab", split_axis=1, concat_axis=2, tiled=True)
    imag_part = lax.all_to_all(col_imag, "slab", split_axis=1, concat_axis=2, tiled=True)
    real_part, imag_part = transform(real_part, imag_part, along_y, cos_t, sin_t, 1.0)
    real_part, imag_part = transform(real_part, imag_part, along_x, cos_t, sin_t, 1.0)
    scale_inv = 1.0 / float(grid_len * grid_len * grid_len)
    shaped = (orb_count, src_count // 2, plane_count, grid_len, grid_len)
    pot_even = real_part.reshape(shaped) * scale_inv
    pot_odd = imag_part.reshape(shaped) * scale_inv
    weighted_even = source[0::2] * occupation[0::2][:, None, None, None]
    weighted_odd = source[1::2] * occupation[1::2][:, None, None, None]
    summed = jnp.sum(pot_even * weighted_even[None], axis=1) + jnp.sum(
        pot_odd * weighted_odd[None], axis=1
    )
    return -summed


def halves(value):
    top = value.astype(BF16)
    return (top, (value - top.astype(F32)).astype(BF16))


def cas_tables(grid_len):
    indices = jnp.arange(grid_len, dtype=jnp.int32)
    product = indices[:, None] * indices[None, :] % grid_len
    angles = product.astype(F32) * (2.0 * math.pi / grid_len)
    table = jnp.cos(angles) + jnp.sin(angles)
    top = lax.reduce_precision(table, 8, 7)
    high, low = (top.astype(BF16), (table - top).astype(BF16))
    zero = jnp.zeros_like(high)
    right = jnp.block([[high, low], [high, zero]])
    left = jnp.block([[high, high], [low, zero]])
    return (right, left)


def times_table(rows, right):
    grid_len = rows.shape[1]
    both = jnp.dot(jnp.concatenate(halves(rows), 1), right, preferred_element_type=F32)
    return both[:, :grid_len] + both[:, grid_len:]


def table_times(left, cols):
    grid_len = cols.shape[0]
    both = jnp.dot(left, jnp.concatenate(halves(cols), 0), preferred_element_type=F32)
    return both[:grid_len] + both[grid_len:]


def beside(rows, count):
    size = rows.shape[0] // count
    return jnp.concatenate([rows[k * size : (k + 1) * size] for k in range(count)], 1)


def below(cols, count):
    size = cols.shape[1] // count
    return jnp.concatenate([cols[:, k * size : (k + 1) * size] for k in range(count)], 0)


STEP = 16
PAD = 8
PARTS = 2


def exchange_kernel(grid_len, slots, layout, last, where_ref, occ_ref, gx_ref, gz_ref, right_ref, left_ref, *refs):
    refs = list(refs)
    n = grid_len
    slot_len = n // slots
    slab_len = slot_len // 2
    part_len = slab_len // PARTS
    res_refs = [[refs.pop(0) for _ in range(slots)] for _ in range(2)]
    src_refs = [(refs.pop(0), *place) for place in layout]
    old_ref = refs.pop(0) if last else None
    out_refs = [refs.pop(0) for _ in range(3 if last else 1)]
    res, src, work, acc, res_sem, src_sem, old_sem, out_sem = refs
    core, parity = (where_ref[0], where_ref[1])

    def res_copy(ref, kind, slot):
        side = core if kind == 0 else 1 - core
        start = slot * slot_len + side * slab_len
        return pltpu.make_async_copy(ref, res.at[pl.ds(start, slab_len)], res_sem.at[kind, slot])

    def src_copy(ref, slot, kind, part):
        side = parity if kind == 0 else 1 - parity
        start = slot * slot_len + side * slab_len + part * part_len
        return pltpu.make_async_copy(ref, src.at[pl.ds(start, part_len)], src_sem.at[slot, kind, part])

    def old_copy(slot):
        span = pl.ds(slot * slot_len, slot_len)
        return pltpu.make_async_copy(old_ref.at[span], acc.at[span], old_sem.at[slot])

    def out_copies(slot):
        if not last:
            span = pl.ds(slot * slot_len, slot_len)
            return [pltpu.make_async_copy(acc.at[span], out_refs[0].at[span], out_sem.at[slot, 0])]
        keep = acc.at[pl.ds(slot * slot_len + core * slab_len, slab_len)]
        give = acc.at[pl.ds(slot * slot_len + (1 - core) * slab_len, slab_len)]
        target = out_refs[1 if slot % 2 == 1 else 2].at[slot // 2]
        return [
            pltpu.make_async_copy(keep, out_refs[0].at[slot], out_sem.at[slot, 0]),
            pltpu.make_async_copy(give, target, out_sem.at[slot, 1]),
        ]

    for slot in range(slots):
        for kind in range(2):
            res_copy(res_refs[kind][slot], kind, slot).start()
        for ref, first_slot, slot_count, kind, part in src_refs:
            if first_slot <= slot < first_slot + slot_count:
                src_copy(ref.at[slot - first_slot], slot, kind, part).start()
    if last:
        for slot in range(slots):
            old_copy(slot).start()
    right = right_ref[...]
    left = left_ref[...]
    scale = 4.0 * math.pi / float(n) ** 3
    steps = slot_len // STEP
    weight = -occ_ref[0]

    def forward(i, carry):
        slot = i // steps

        @pl.when(i % steps == 0)
        def _():
            for kind in range(2):
                res_copy(res_refs[0][0], kind, slot).wait()
                for part in range(PARTS):
                    src_copy(src_refs[0][0].at[0], slot, kind, part).wait()

        z = i * STEP
        value = (res[pl.ds(z, STEP)] * src[pl.ds(z, STEP)]).reshape(STEP * n, n)
        value = table_times(left, beside(times_table(value, right), STEP))
        for k in range(STEP):
            work[pl.ds((z + k) * (n + PAD), n), :] = value[:, k * n : (k + 1) * n]
        return carry

    lax.fori_loop(0, n // STEP, forward, 0)

    def columns(i, carry):
        y = i * STEP
        value = jnp.concatenate([work[pl.ds(y + k, n, stride=n + PAD), :] for k in range(STEP)], 1)
        value = table_times(left, value)
        base = gz_ref[...] + (gx_ref[...] + KAPPA_SQ)
        value = jnp.concatenate(
            [
                value[:, k * n : (k + 1) * n] * (scale / (base + gz_ref[pl.ds(y + k, 1), :]))
                for k in range(STEP)
            ],
            1,
        )
        value = table_times(left, value)
        for k in range(STEP):
            work[pl.ds(y + k, n, stride=n + PAD), :] = value[:, k * n : (k + 1) * n]
        return carry

    lax.fori_loop(0, n // STEP, columns, 0)

    def backward(i, carry):
        turn = i // steps
        half = slots // 2
        slot = jnp.where(turn < half, 2 * turn + 1, 2 * (turn - half))
        if last:

            @pl.when(i % steps == 0)
            def _():
                old_copy(slot).wait()

        z = (slot * steps + i % steps) * STEP
        value = jnp.concatenate([work[pl.ds((z + k) * (n + PAD), n), :] for k in range(STEP)], 1)
        value = times_table(below(table_times(left, value), STEP), right).reshape(STEP, n, n)
        value = value * (src[pl.ds(z, STEP)] * weight)
        if last:
            value = value + acc[pl.ds(z, STEP)]
        acc[pl.ds(z, STEP)] = value
        for done in range(slots):

            @pl.when((i % steps == steps - 1) & (slot == done))
            def _(done=done):
                for copy in out_copies(done):
                    copy.start()

        return carry

    lax.fori_loop(0, n // STEP, backward, 0)
    for slot in range(slots):
        for copy in out_copies(slot):
            copy.wait()


def exchange(where, occ, res_pieces, src_pieces, old, tables, waves):
    right, left = tables
    slots = len(res_pieces[0])
    slab_len, n, _ = res_pieces[0][0].shape
    last = old is not None
    any_spec = pl.BlockSpec(memory_space=pl.ANY)
    vmem_spec = pl.BlockSpec(memory_space=pltpu.VMEM)
    smem_spec = pl.BlockSpec(memory_space=pltpu.SMEM)
    layout = [place for _, *place in src_pieces]
    arrays = [*res_pieces[0], *res_pieces[1], *[array for array, *_ in src_pieces]]
    if last:
        arrays.append(old)
        shapes = [(slots, slab_len, n, n), (slots // 2, slab_len, n, n), (slots // 2, slab_len, n, n)]
    else:
        shapes = [(n, n, n)]
    return pl.pallas_call(
        functools.partial(exchange_kernel, n, slots, layout, last),
        out_shape=[jax.ShapeDtypeStruct(shape, F32) for shape in shapes],
        in_specs=[smem_spec] * 2 + [vmem_spec] * 4 + [any_spec] * len(arrays),
        out_specs=[any_spec] * len(shapes),
        scratch_shapes=[
            pltpu.VMEM((n, n, n), F32),
            pltpu.VMEM((n, n, n), F32),
            pltpu.VMEM((n * (n + PAD), n), F32),
            pltpu.VMEM((n, n, n), F32),
            pltpu.SemaphoreType.DMA((2, slots)),
            pltpu.SemaphoreType.DMA((slots, 2, PARTS)),
            pltpu.SemaphoreType.DMA((slots,)),
            pltpu.SemaphoreType.DMA((slots, 2)),
        ],
        compiler_params=pltpu.CompilerParams(vmem_limit_bytes=48 * 2**20),
        cost_estimate=pl.CostEstimate(
            flops=72 * n**4, bytes_accessed=4 * n**3 * (5 if last else 3), transcendentals=0
        ),
        name="exchange",
    )(where, occ.reshape(1), waves[None, :], jnp.broadcast_to(waves[:, None], (n, n)), right, left, *arrays)


def whole_grids(resident, blocks, occupation):
    count_res, slab_len, n, _ = resident.shape
    planes = lax.axis_size("slab") // 2
    names = ("band", "slab")
    coords = [
        (x, c, z, y) for x in range(2) for c in range(2) for z in range(planes) for y in range(2)
    ]

    def flat(x, c, z, y):
        return ((x * 2 + c) * planes + z) * 2 + y

    def send(value, rule):
        pairs = []
        for coord in coords:
            target = rule(*coord)
            if target is not None:
                pairs.append((flat(*coord), flat(*target)))
        return lax.ppermute(value, names, pairs)

    band, slab = (lax.axis_index("band"), lax.axis_index("slab"))
    c, z, y = (band % 2, slab // 2, slab % 2)

    def swap_x(v):
        return send(v, lambda x, c, z, y: (1 - x, c, z, y))

    def swap_c(v):
        return send(v, lambda x, c, z, y: (x, 1 - c, z, y))

    def swap_y(v):
        return send(v, lambda x, c, z, y: (x, c, z, 1 - y))

    def turn_cy(v):
        return send(v, lambda x, c, z, y: (x, y, z, c))

    def pick(values, index):
        out = values[0]
        for k in range(1, len(values)):
            out = jnp.where(index == k, values[k], out)
        return out

    part_len = slab_len // PARTS
    own = []
    for part in range(PARTS):
        rows = slice(part * part_len, (part + 1) * part_len)
        quads = [lax.dynamic_index_in_dim(blocks, band, 0, False)[rows]]
        for other in range(1, 4):
            dx, dc = (other // 2, other % 2)
            value = lax.dynamic_index_in_dim(blocks, band ^ other, 0, False)[rows]
            quads.append(send(value, lambda x, c, z, y, dx=dx, dc=dc: (x ^ dx, c ^ dc, z, y)))
        slots = [pick(quads, z ^ band)]
        for step in range(1, planes):
            value = pick(quads, ((z + step) % planes) ^ band)
            slots.append(send(value, lambda x, c, z, y, step=step: (x, c, (z + step) % planes, y)))
        own.append(jnp.stack([slots[0], *slots[:0:-1]]))

    residents = []
    for r in range(count_res):
        piece = turn_cy(resident[r])
        downs, ups = ([], [])
        down = up = piece
        for step in range(1, planes):
            if r == 0 and step == 2:
                down, up, _ = lax.optimization_barrier((down, up, own[-1]))
            if r > 0 and step == 1:
                down, up, earlier = lax.optimization_barrier((down, up, earlier))
            down = send(down, lambda x, c, z, y: (x, c, z - 1, y) if 1 <= z <= planes - step else None)
            up = send(up, lambda x, c, z, y: (x, c, z + 1, y) if step - 1 <= z < planes - 1 else None)
            downs.append(down)
            ups.append(up)
        earlier = downs[1]
        slots = [piece]
        for step in range(1, planes):
            slots.append(jnp.where(z + step < planes, downs[step - 1], ups[planes - step - 1]))
        residents.append([slots, [swap_c(v) for v in slots]])

    near, far = ([], [])
    half = planes // 2
    for part in range(PARTS):
        beside_y = swap_y(own[part])
        beside_x = swap_x(own[part])
        low = swap_y(beside_x[:half])
        high = swap_x(beside_y[half:])
        near += [(own[part], 0, planes, 0, part), (beside_y, 0, planes, 1, part)]
        far += [
            (beside_x, 0, planes, 0, part),
            (low, 0, half, 1, part),
            (high, half, half, 1, part),
        ]

    occ = [lax.dynamic_index_in_dim(occupation, 4 * z + (band ^ other), 0, False) for other in (0, 2)]
    where = jnp.stack([c, y]).astype(jnp.int32)
    waves = wave_of(jnp.arange(n, dtype=jnp.int32), n) ** 2
    tables = cas_tables(n)
    rows, ties = ([], [where, where])
    for r in range(count_res):
        (old,) = exchange(ties[0], occ[0], residents[r], near, None, tables, waves)
        keep, odd, even = exchange(ties[1], occ[1], residents[r], far, old, tables, waves)
        odd, even = (swap_c(odd), swap_c(even))

        terms = {}
        for part, array in ((1, odd), (0, even)):
            slots = range(part, planes, 2)
            sums = [keep[slot] + array[slot // 2] for slot in slots]
            terms.update(zip(slots, lax.optimization_barrier(sums)))

        down = up = None
        for step in range(1, planes):
            low, high = (terms[step], terms[planes - step])
            if step > 1:
                low, high = (low + down, high + up)
            if r + 1 < count_res and step < planes - 1:
                low, high, ties[step - 1] = lax.optimization_barrier((low, high, where))
            down = send(low, lambda x, c, z, y: (x, c, z - 1, y) if z >= max(planes - step, 1) else None)
            up = send(high, lambda x, c, z, y: (x, c, z + 1, y) if z <= min(step - 1, planes - 2) else None)
        rows.append(turn_cy(terms[0] + down + up))
    return jnp.stack(rows)


def per_device(resident, blocks, occupation):
    if (
        lax.axis_size("band") == 4
        and lax.axis_size("slab") == 8
        and resident.shape[0] == 2
        and blocks.shape[0] == 4
        and resident.shape[1] % STEP == 0
    ):
        return whole_grids(resident, blocks, occupation)
    return sliced_grids(resident, blocks, occupation)


def solution(mesh):
    placed = (P("band", "slab", None, None), P("band", "slab", None, None), P())
    return jax.shard_map(
        per_device,
        mesh=mesh,
        in_specs=placed,
        out_specs=P("band", "slab", None, None),
        check_vma=False,
    )
```

profile of v0, /device:TPU:17, one launch (start us, length us, event | category | flops | bytes accessed | tf_op | source)
XLA Modules:
  0.0 575.8 jit_solution(17636981074874935541)
XLA Ops:
  0.0 3.3 dynamic-slice_bitcast_fusion.1
  3.3 1.8 collective-permute-start.17
  6.5 3.2 collective-permute-start
  9.7 1.6 collective-permute-start.3
  11.3 6.5 %collective-permute-done.17 = f32[8,128,128]{2,1,0:T(8,128)} collective-permute-done((f32[8,128,128]{2,1,0:T(8,128)S(1)}, f32[8,128,128]{2,1,0:T(8,128)}, u32[]{:S(2)}, u32[]{:S(2)}) %collective-permute-start.17) | collective-permute-done | bytes 524320 | tf_op jit(solution)/shard_map/ppermute | solution.py:325
  19.1 10.0 %collective-permute-done.18 = f32[8,128,128]{2,1,0:T(8,128)} collective-permute-done((f32[8,128,128]{2,1,0:T(8,128)S(1)}, f32[8,128,128]{2,1,0:T(8,128)}, u32[]{:S(2)}, u32[]{:S(2)}) %collective-permute-start.18) | collective-permute-done | bytes 524320 | tf_op jit(solution)/shard_map/ppermute | solution.py:325
  29.5 1.8 select_bitcast_fusion
  31.6 8.7 %collective-permute-done.3 = f32[8,128,128]{2,1,0:T(8,128)S(1)} collective-permute-done((f32[8,128,128]{2,1,0:T(8,128)}, f32[8,128,128]{2,1,0:T(8,128)S(1)}, u32[]{:S(2)}, u32[]{:S(2)}) %collective-permute-start.3) | collective-permute-done | bytes 524320 | tf_op jit(solution)/shard_map/ppermute | solution.py:325
  40.3 11.1 %collective-permute-done.4 = f32[8,128,128]{2,1,0:T(8,128)S(1)} collective-permute-done((f32[8,128,128]{2,1,0:T(8,128)S(1)}, f32[8,128,128]{2,1,0:T(8,128)S(1)}, u32[]{:S(2)}, u32[]{:S(2)}) %collective-permute-start.4) | collective-permute-done | bytes 524320 | tf_op jit(solution)/shard_map/ppermute | solution.py:325
  51.4 1.3 collective-permute-start.22
  52.7 2.1 collective-permute-start.1
  54.8 3.3 collective-permute-start.2
  58.1 1.5 select_bitcast_fusion.1
  59.6 16.9 %collective-permute-done.21 = f32[8,128,128]{2,1,0:T(8,128)S(1)} collective-permute-done((f32[8,128,128]{2,1,0:T(8,128)S(1)}, f32[8,128,128]{2,1,0:T(8,128)S(1)}, u32[]{:S(2)}, u32[]{:S(2)}) %collective-permute-start.21) | collective-permute-done | bytes 524320 | tf_op jit(solution)/shard_map/ppermute | solution.py:325
  76.6 4.4 collective-permute-done.22
  80.9 1.5 pad_maximum_fusion.1.refs_8_
  82.4 54.7 %collective-permute-done.8 = f32[8,128,128]{2,1,0:T(8,128)S(1)} collective-permute-done((f32[8,128,128]{2,1,0:T(8,128)S(1)}, f32[8,128,128]{2,1,0:T(8,128)S(1)}, u32[]{:S(2)}, u32[]{:S(2)}) %collective-permute-start.8) | collective-permute-done | bytes 524320 | tf_op jit(solution)/shard_map/ppermute | solution.py:325
  138.3 5.7 collective-permute-done.7
  144.0 1.4 pad_maximum_fusion.refs_10_
  145.5 5.6 collective-permute-start.11
  151.1 2.6 collective-permute-start.9
  153.6 1.3 collective-permute-start.25
  155.2 17.8 %collective-permute-done.11 = f32[16,128,128]{2,1,0:T(8,128)S(1)} collective-permute-done((f32[16,128,128]{2,1,0:T(8,128)S(1)}, f32[16,128,128]{2,1,0:T(8,128)S(1)}, u32[]{:S(2)}, u32[]{:S(2)}) %collective-permute-start.11) | collective-permute-done | bytes 1048608 | tf_op jit(solution)/shard_map/ppermute | solution.py:325
  173.7 3.3 collective-permute-done.9
  178.2 5.9 %collective-permute-done.23.refs_8_ = f32[4,8,128,128]{3,2,1,0:T(8,128)} collective-permute-done((f32[4,8,128,128]{3,2,1,0:T(8,128)}, f32[4,8,128,128]{3,2,1,0:T(8,128)}, u32[]{:S(2)}, u32[]{:S(2)}) %collective-permute-start.23) | collective-permute-done | bytes 2097184 | tf_op jit(solution)/shard_map/ppermute | solution.py:325
  184.1 5.4 collective-permute-start.40
  190.5 2.3 collective-permute-start.10
  192.8 2.3 slice.152
  195.2 1.5 broadcast_select_fusion.3.refs_2_
  197.2 60.3 %collective-permute-done.40.refs_0_ = f32[16,128,128]{2,1,0:T(8,128)S(1)} collective-permute-done((f32[16,128,128]{2,1,0:T(8,128)}, f32[16,128,128]{2,1,0:T(8,128)S(1)}, u32[]{:S(2)}, u32[]{:S(2)}) %collective-permute-start.40) | collective-permute-done | bytes 1048608 | tf_op jit(solution)/shard_map/ppermute | solution.py:325
  258.0 1.5 collective-permute-start.24
  261.5 1.3 slice.153
  262.8 1.4 slice.154
  264.2 1.3 slice.155
  266.9 15.9 %collective-permute-done.24.refs_9_ = f32[2,8,128,128]{3,2,1,0:T(8,128)} collective-permute-done((f32[2,8,128,128]{3,2,1,0:T(8,128)}, f32[2,8,128,128]{3,2,1,0:T(8,128)}, u32[]{:S(2)}, u32[]{:S(2)}) %collective-permute-start.24) | collective-permute-done | bytes 1048608 | tf_op jit(solution)/shard_map/ppermute | solution.py:325
  284.1 1.9 collective-permute-start.42
  286.0 3.7 collective-permute-start.41
  289.8 25.0 %exchange.4.refs_14_ = f32[128,128,128]{2,1,0:T(8,128)} custom-call(s32[2]{0:T(128)S(1)} %pad_add_fusion.where_ref, f32[1]{0:T(128)} %get-tuple-element.87.occ_ref, f32[1,128]{1,0:T(1,128)S(1)} %fusion.21.gx_ref, f32[128,128]{1,0:T(8,128)S(1)} %broadcast_in_dim.8.gz_ref, bf16[256,256]{1,0:T(8,128)(2,1)S(1)} %get-tuple-element.86.right_ref, ...), custom_call_target="tpu_custom_call" | custom-call | flops 19327352832 | bytes 25165824 | tf_op jit(solution)/shard_map/exchange/pallas_call | solution.py:285
  314.8 1.9 collective-permute-start.43
  316.7 3.5 collective-permute-start.45
  321.2 25.0 %exchange.5 = (f32[4,16,128,128]{3,2,1,0:T(8,128)}, f32[2,16,128,128]{3,2,1,0:T(8,128)}, f32[2,16,128,128]{3,2,1,0:T(8,128)}) custom-call(s32[2]{0:T(128)S(1)} %pad_add_fusion.where_ref, f32[1]{0:T(128)} %get-tuple-element.88.occ_ref, f32[1,128]{1,0:T(1,128)S(1)} %fusion.21.gx_ref, f32[128,128]{1,0:T(8,128)S(1)} %broadcast_in_dim.8.gz_ref, ...), custom_call_target="tpu_custom_call" | custom-call | flops 19327352832 | bytes 41943040 | tf_op jit(solution)/shard_map/exchange/pallas_call | solution.py:285
  346.2 2.8 collective-permute-start.31
  349.0 1.3 collective-permute-start.44
  352.0 21.0 %collective-permute-done.44 = f32[16,128,128]{2,1,0:T(8,128)S(1)} collective-permute-done((f32[16,128,128]{2,1,0:T(8,128)S(1)}, f32[16,128,128]{2,1,0:T(8,128)S(1)}, u32[]{:S(2)}, u32[]{:S(2)}) %collective-permute-start.44) | collective-permute-done | bytes 1048608 | tf_op jit(solution)/shard_map/ppermute | solution.py:325
  381.0 24.5 %exchange.6.refs_14_ = f32[128,128,128]{2,1,0:T(8,128)} custom-call(s32[2]{0:T(128)S(1)} %pad_add_fusion.where_ref, f32[1]{0:T(128)} %get-tuple-element.87.occ_ref, f32[1,128]{1,0:T(1,128)S(1)} %fusion.21.gx_ref, f32[128,128]{1,0:T(8,128)S(1)} %broadcast_in_dim.8.gz_ref, bf16[256,256]{1,0:T(8,128)(2,1)S(1)} %get-tuple-element.86.right_ref, ...), custom_call_target="tpu_custom_call" | custom-call | flops 19327352832 | bytes 25165824 | tf_op jit(solution)/shard_map/exchange/pallas_call | solution.py:285
  405.8 24.4 %exchange.7 = (f32[4,16,128,128]{3,2,1,0:T(8,128)}, f32[2,16,128,128]{3,2,1,0:T(8,128)}, f32[2,16,128,128]{3,2,1,0:T(8,128)}) custom-call(s32[2]{0:T(128)S(1)} %pad_add_fusion.where_ref, f32[1]{0:T(128)} %get-tuple-element.88.occ_ref, f32[1,128]{1,0:T(1,128)S(1)} %fusion.21.gx_ref, f32[128,128]{1,0:T(8,128)S(1)} %broadcast_in_dim.8.gz_ref, ...), custom_call_target="tpu_custom_call" | custom-call | flops 19327352832 | bytes 41943040 | tf_op jit(solution)/shard_map/exchange/pallas_call | solution.py:285
  430.8 3.9 collective-permute-done.51
  434.7 3.0 collective-permute-done.52
  437.7 2.9 fusion.2
  442.6 1.9 collective-permute-start.35
  445.9 21.6 %collective-permute-done.53 = f32[16,128,128]{2,1,0:T(8,128)S(1)} collective-permute-done((f32[16,128,128]{2,1,0:T(8,128)S(1)}, f32[16,128,128]{2,1,0:T(8,128)S(1)}, u32[]{:S(2)}, u32[]{:S(2)}) %collective-permute-start.53) | collective-permute-done | bytes 1048608 | tf_op jit(solution)/shard_map/ppermute | solution.py:325
  467.6 1.9 collective-permute-start.54
  470.9 19.0 %collective-permute-done.35 = f32[16,128,128]{2,1,0:T(8,128)S(1)} collective-permute-done((f32[16,128,128]{2,1,0:T(8,128)S(1)}, f32[16,128,128]{2,1,0:T(8,128)S(1)}, u32[]{:S(2)}, u32[]{:S(2)}) %collective-permute-start.35) | collective-permute-done | bytes 1048608 | tf_op jit(solution)/shard_map/ppermute | solution.py:325
  490.0 1.9 collective-permute-start.36
  492.1 3.4 collective-permute-start.38
  495.5 16.8 %collective-permute-done.54 = f32[16,128,128]{2,1,0:T(8,128)S(1)} collective-permute-done((f32[16,128,128]{2,1,0:T(8,128)S(1)}, f32[16,128,128]{2,1,0:T(8,128)S(1)}, u32[]{:S(2)}, u32[]{:S(2)}) %collective-permute-start.54) | collective-permute-done | bytes 1048608 | tf_op jit(solution)/shard_map/ppermute | solution.py:325
  512.5 1.9 collective-permute-start.55
  514.6 3.4 collective-permute-start.58
  518.0 16.9 %collective-permute-done.36 = f32[16,128,128]{2,1,0:T(8,128)S(1)} collective-permute-done((f32[16,128,128]{2,1,0:T(8,128)S(1)}, f32[16,128,128]{2,1,0:T(8,128)S(1)}, u32[]{:S(2)}, u32[]{:S(2)}) %collective-permute-start.36) | collective-permute-done | bytes 1048608 | tf_op jit(solution)/shard_map/ppermute | solution.py:325
  535.1 4.7 collective-permute-start.39
  539.8 17.5 %collective-permute-done.55 = f32[16,128,128]{2,1,0:T(8,128)S(1)} collective-permute-done((f32[16,128,128]{2,1,0:T(8,128)S(1)}, f32[16,128,128]{2,1,0:T(8,128)S(1)}, u32[]{:S(2)}, u32[]{:S(2)}) %collective-permute-start.55) | collective-permute-done | bytes 1048608 | tf_op jit(solution)/shard_map/ppermute | solution.py:325
  557.5 4.3 collective-permute-start.59
  561.9 12.5 %collective-permute-done.59 = f32[16,128,128]{2,1,0:T(8,128)S(1)} collective-permute-done((f32[16,128,128]{2,1,0:T(8,128)S(1)}, f32[16,128,128]{2,1,0:T(8,128)S(1)}, u32[]{:S(2)}, u32[]{:S(2)}) %collective-permute-start.59) | collective-permute-done | bytes 1048608 | tf_op jit(solution)/shard_map/ppermute | solution.py:325
  574.3 1.5 pad_maximum_fusion.2
  (124 shorter events, 30.6 us)
Async XLA Ops:
  3.3 14.6 %collective-permute-start.17 = (f32[8,128,128]{2,1,0:T(8,128)S(1)}, f32[8,128,128]{2,1,0:T(8,128)}, u32[]{:S(2)}, u32[]{:S(2)}) collective-permute-start(f32[8,128,128]{2,1,0:T(8,128)S(1)} %get-tuple-element.78), channel_id=1, source_target_pairs={{0,24},{1,25},{2,26},{3,27},{4,28},{5,29},{6,30},{7,31},{8,16},{9,... | collective-permute-start | bytes 1572872 | tf_op jit(solution)/shard_map/ppermute | solution.py:325
  5.0 24.0 %collective-permute-start.18 = (f32[8,128,128]{2,1,0:T(8,128)S(1)}, f32[8,128,128]{2,1,0:T(8,128)}, u32[]{:S(2)}, u32[]{:S(2)}) collective-permute-start(f32[8,128,128]{2,1,0:T(8,128)S(1)} %get-tuple-element.77), channel_id=1, source_target_pairs={{0,16},{1,17},{2,18},{3,19},{4,20},{5,21},{6,22},{7,23},{8,24},{9,... | collective-permute-start | bytes 1572872 | tf_op jit(solution)/shard_map/ppermute | solution.py:325
  6.5 46.2 %collective-permute-start = (f32[16,128,128]{2,1,0:T(8,128)S(1)}, f32[16,128,128]{2,1,0:T(8,128)}, u32[]{:S(2)}, u32[]{:S(2)}) collective-permute-start(f32[16,128,128]{2,1,0:T(8,128)S(1)} %get-tuple-element.80), channel_id=1, source_target_pairs={{0,0},{1,8},{2,2},{3,10},{4,4},{5,12},{6,6},{7,14},{8,1},{9,9},{10... | collective-permute-start | bytes 3145736 | tf_op jit(solution)/shard_map/ppermute | solution.py:325
  9.7 19.9 %collective-permute-start.19 = (f32[8,128,128]{2,1,0:T(8,128)}, f32[8,128,128]{2,1,0:T(8,128)}, u32[]{:S(2)}, u32[]{:S(2)}) collective-permute-start(f32[8,128,128]{2,1,0:T(8,128)} %get-tuple-element.73), channel_id=1, source_target_pairs={{0,8},{1,9},{2,10},{3,11},{4,12},{5,13},{6,14},{7,15},{8,0},{9,1},... | collective-permute-start | bytes 1572872 | tf_op jit(solution)/shard_map/ppermute | solution.py:325
  9.7 30.5 %collective-permute-start.3 = (f32[8,128,128]{2,1,0:T(8,128)}, f32[8,128,128]{2,1,0:T(8,128)S(1)}, u32[]{:S(2)}, u32[]{:S(2)}) collective-permute-start(f32[8,128,128]{2,1,0:T(8,128)} %get-tuple-element.76), channel_id=1, source_target_pairs={{0,24},{1,25},{2,26},{3,27},{4,28},{5,29},{6,30},{7,31},{8,16},{9,... | collective-permute-start | bytes 1572872 | tf_op jit(solution)/shard_map/ppermute | solution.py:325
  17.8 33.6 %collective-permute-start.4 = (f32[8,128,128]{2,1,0:T(8,128)S(1)}, f32[8,128,128]{2,1,0:T(8,128)S(1)}, u32[]{:S(2)}, u32[]{:S(2)}) collective-permute-start(f32[8,128,128]{2,1,0:T(8,128)S(1)} %get-tuple-element.75), channel_id=1, source_target_pairs={{0,16},{1,17},{2,18},{3,19},{4,20},{5,21},{6,22},{7,23},{8,24},{9,... | collective-permute-start | bytes 1572872 | tf_op jit(solution)/shard_map/ppermute | solution.py:325
  29.1 25.7 %collective-permute-start.5 = (f32[8,128,128]{2,1,0:T(8,128)S(1)}, f32[8,128,128]{2,1,0:T(8,128)}, u32[]{:S(2)}, u32[]{:S(2)}) collective-permute-start(f32[8,128,128]{2,1,0:T(8,128)S(1)} %get-tuple-element.74), channel_id=1, source_target_pairs={{0,8},{1,9},{2,10},{3,11},{4,12},{5,13},{6,14},{7,15},{8,0},{9,1},... | collective-permute-start | bytes 1572872 | tf_op jit(solution)/shard_map/ppermute | solution.py:325
  31.4 28.2 %collective-permute-start.20 = (f32[8,128,128]{2,1,0:T(8,128)S(1)}, f32[8,128,128]{2,1,0:T(8,128)S(1)}, u32[]{:S(2)}, u32[]{:S(2)}) collective-permute-start(f32[8,128,128]{2,1,0:T(8,128)S(1)} %get-tuple-element.64), channel_id=1, source_target_pairs={{0,6},{1,7},{2,0},{3,1},{4,2},{5,3},{6,4},{7,5},{8,14},{9,15},{10,... | collective-permute-start | bytes 1572872 | tf_op jit(solution)/shard_map/ppermute | solution.py:325
  40.3 36.3 %collective-permute-start.21 = (f32[8,128,128]{2,1,0:T(8,128)S(1)}, f32[8,128,128]{2,1,0:T(8,128)S(1)}, u32[]{:S(2)}, u32[]{:S(2)}) collective-permute-start(f32[8,128,128]{2,1,0:T(8,128)S(1)} %get-tuple-element.63), channel_id=1, source_target_pairs={{0,4},{1,5},{2,6},{3,7},{4,0},{5,1},{6,2},{7,3},{8,12},{9,13},{10,... | collective-permute-start | bytes 1572872 | tf_op jit(solution)/shard_map/ppermute | solution.py:325
  51.4 29.5 %collective-permute-start.22 = (f32[8,128,128]{2,1,0:T(8,128)S(1)}, f32[8,128,128]{2,1,0:T(8,128)S(1)}, u32[]{:S(2)}, u32[]{:S(2)}) collective-permute-start(f32[8,128,128]{2,1,0:T(8,128)S(1)} %get-tuple-element.62), channel_id=1, source_target_pairs={{0,2},{1,3},{2,4},{3,5},{4,6},{5,7},{6,0},{7,1},{8,10},{9,11},{10,... | collective-permute-start | bytes 1572872 | tf_op jit(solution)/shard_map/ppermute | solution.py:325
  52.7 92.7 %collective-permute-start.1 = (f32[16,128,128]{2,1,0:T(8,128)}, f32[16,128,128]{2,1,0:T(8,128)S(1)}, u32[]{:S(2)}, u32[]{:S(2)}) collective-permute-start(f32[16,128,128]{2,1,0:T(8,128)} %collective-permute-done.refs_0_), channel_id=1, source_target_pairs={{2,0},{3,1},{4,2},{5,3},{6,4},{7,5},{10,8},{11,9},{12,10},{13,11},... | collective-permute-start | bytes 3145736 | tf_op jit(solution)/shard_map/ppermute | solution.py:325
  54.8 90.6 %collective-permute-start.2 = (f32[16,128,128]{2,1,0:T(8,128)}, f32[16,128,128]{2,1,0:T(8,128)S(1)}, u32[]{:S(2)}, u32[]{:S(2)}) collective-permute-start(f32[16,128,128]{2,1,0:T(8,128)} %collective-permute-done.refs_0_), channel_id=1, source_target_pairs={{0,2},{1,3},{2,4},{3,5},{4,6},{5,7},{8,10},{9,11},{10,12},{11,13},... | collective-permute-start | bytes 3145736 | tf_op jit(solution)/shard_map/ppermute | solution.py:325
  59.6 77.5 %collective-permute-start.8 = (f32[8,128,128]{2,1,0:T(8,128)S(1)}, f32[8,128,128]{2,1,0:T(8,128)S(1)}, u32[]{:S(2)}, u32[]{:S(2)}) collective-permute-start(f32[8,128,128]{2,1,0:T(8,128)S(1)} %get-tuple-element.66), channel_id=1, source_target_pairs={{0,2},{1,3},{2,4},{3,5},{4,6},{5,7},{6,0},{7,1},{8,10},{9,11},{10,... | collective-permute-start | bytes 1572872 | tf_op jit(solution)/shard_map/ppermute | solution.py:325
  76.6 61.7 %collective-permute-start.6 = (f32[8,128,128]{2,1,0:T(8,128)S(1)}, f32[8,128,128]{2,1,0:T(8,128)S(1)}, u32[]{:S(2)}, u32[]{:S(2)}) collective-permute-start(f32[8,128,128]{2,1,0:T(8,128)S(1)} %get-tuple-element.68), channel_id=1, source_target_pairs={{0,6},{1,7},{2,0},{3,1},{4,2},{5,3},{6,4},{7,5},{8,14},{9,15},{10,... | collective-permute-start | bytes 1572872 | tf_op jit(solution)/shard_map/ppermute | solution.py:325
  80.9 63.1 %collective-permute-start.7 = (f32[8,128,128]{2,1,0:T(8,128)S(1)}, f32[8,128,128]{2,1,0:T(8,128)S(1)}, u32[]{:S(2)}, u32[]{:S(2)}) collective-permute-start(f32[8,128,128]{2,1,0:T(8,128)S(1)} %get-tuple-element.67), channel_id=1, source_target_pairs={{0,4},{1,5},{2,6},{3,7},{4,0},{5,1},{6,2},{7,3},{8,12},{9,13},{10,... | collective-permute-start | bytes 1572872 | tf_op jit(solution)/shard_map/ppermute | solution.py:325
  137.1 47.0 %collective-permute-start.23 = (f32[4,8,128,128]{3,2,1,0:T(8,128)}, f32[4,8,128,128]{3,2,1,0:T(8,128)}, u32[]{:S(2)}, u32[]{:S(2)}) collective-permute-start(f32[4,8,128,128]{3,2,1,0:T(8,128)} %pad_maximum_fusion.1.refs_8_), channel_id=1, source_target_pairs={{0,16},{1,17},{2,18},{3,19},{4,20},{5,21},{6,22},{7,23},{8,24},{9,... | collective-permute-start | bytes 6291464 | tf_op jit(solution)/shard_map/ppermute | solution.py:325
  145.4 38.6 %copy-start.4 = (f32[16,128,128]{2,1,0:T(8,128)}, f32[16,128,128]{2,1,0:T(8,128)S(1)}, u32[]{:S(2)}) copy-start(f32[16,128,128]{2,1,0:T(8,128)S(1)} %collective-permute-done.1) | copy-start | bytes 3145732
  145.4 38.6 %copy-start.6 = (f32[16,128,128]{2,1,0:T(8,128)}, f32[16,128,128]{2,1,0:T(8,128)S(1)}, u32[]{:S(2)}) copy-start(f32[16,128,128]{2,1,0:T(8,128)S(1)} %collective-permute-done.2) | copy-start | bytes 3145732
  145.5 27.5 %collective-permute-start.11 = (f32[16,128,128]{2,1,0:T(8,128)S(1)}, f32[16,128,128]{2,1,0:T(8,128)S(1)}, u32[]{:S(2)}, u32[]{:S(2)}) collective-permute-start(f32[16,128,128]{2,1,0:T(8,128)S(1)} %collective-permute-done.1), channel_id=1, source_target_pairs={{2,0},{3,1},{4,2},{5,3},{10,8},{11,9},{12,10},{13,11},{18,16},{19,... | collective-permute-start | bytes 3145736 | tf_op jit(solution)/shard_map/ppermute | solution.py:325
  151.1 26.0 %collective-permute-start.9 = (f32[16,128,128]{2,1,0:T(8,128)S(1)}, f32[16,128,128]{2,1,0:T(8,128)}, u32[]{:S(2)}, u32[]{:S(2)}) collective-permute-start(f32[16,128,128]{2,1,0:T(8,128)S(1)} %collective-permute-done.2), channel_id=1, source_target_pairs={{2,4},{3,5},{4,6},{5,7},{10,12},{11,13},{12,14},{13,15},{18,20},{1... | collective-permute-start | bytes 3145736 | tf_op jit(solution)/shard_map/ppermute | solution.py:325
  153.6 103.8 %collective-permute-start.25 = (f32[4,8,128,128]{3,2,1,0:T(8,128)}, f32[4,8,128,128]{3,2,1,0:T(8,128)}, u32[]{:S(2)}, u32[]{:S(2)}) collective-permute-start(f32[4,8,128,128]{3,2,1,0:T(8,128)} %pad_maximum_fusion.1.refs_8_), channel_id=1, source_target_pairs={{0,1},{1,0},{2,3},{3,2},{4,5},{5,4},{6,7},{7,6},{8,9},{9,8},{10,11... | collective-permute-start | bytes 6291464 | tf_op jit(solution)/shard_map/ppermute | solution.py:325
  155.0 103.0 %collective-permute-start.29 = (f32[4,8,128,128]{3,2,1,0:T(8,128)}, f32[4,8,128,128]{3,2,1,0:T(8,128)}, u32[]{:S(2)}, u32[]{:S(2)}) collective-permute-start(f32[4,8,128,128]{3,2,1,0:T(8,128)} %pad_maximum_fusion.refs_10_), channel_id=1, source_target_pairs={{0,1},{1,0},{2,3},{3,2},{4,5},{5,4},{6,7},{7,6},{8,9},{9,8},{10,11... | collective-permute-start | bytes 6291464 | tf_op jit(solution)/shard_map/ppermute | solution.py:325
  173.0 16.5 %collective-permute-start.12 = (f32[16,128,128]{2,1,0:T(8,128)S(1)}, f32[16,128,128]{2,1,0:T(8,128)S(1)}, u32[]{:S(2)}, u32[]{:S(2)}) collective-permute-start(f32[16,128,128]{2,1,0:T(8,128)S(1)} %collective-permute-done.11), channel_id=1, source_target_pairs={{2,0},{3,1},{10,8},{11,9},{18,16},{19,17},{26,24},{27,25}} | collective-permute-start | bytes 3145736 | tf_op jit(solution)/shard_map/ppermute | solution.py:325
  177.0 83.3 %collective-permute-start.27 = (f32[4,8,128,128]{3,2,1,0:T(8,128)}, f32[4,8,128,128]{3,2,1,0:T(8,128)}, u32[]{:S(2)}, u32[]{:S(2)}) collective-permute-start(f32[4,8,128,128]{3,2,1,0:T(8,128)} %pad_maximum_fusion.refs_10_), channel_id=1, source_target_pairs={{0,16},{1,17},{2,18},{3,19},{4,20},{5,21},{6,22},{7,23},{8,24},{9,... | collective-permute-start | bytes 6291464 | tf_op jit(solution)/shard_map/ppermute | solution.py:325
  184.1 73.4 %collective-permute-start.40 = (f32[16,128,128]{2,1,0:T(8,128)}, f32[16,128,128]{2,1,0:T(8,128)S(1)}, u32[]{:S(2)}, u32[]{:S(2)}) collective-permute-start(f32[16,128,128]{2,1,0:T(8,128)} %get-tuple-element.79), channel_id=1, source_target_pairs={{0,0},{1,8},{2,2},{3,10},{4,4},{5,12},{6,6},{7,14},{8,1},{9,9},{10... | collective-permute-start | bytes 3145736 | tf_op jit(solution)/shard_map/ppermute | solution.py:325
  190.5 68.9 %collective-permute-start.10 = (f32[16,128,128]{2,1,0:T(8,128)}, f32[16,128,128]{2,1,0:T(8,128)}, u32[]{:S(2)}, u32[]{:S(2)}) collective-permute-start(f32[16,128,128]{2,1,0:T(8,128)} %collective-permute-done.9), channel_id=1, source_target_pairs={{4,6},{5,7},{12,14},{13,15},{20,22},{21,23},{28,30},{29,31}} | collective-permute-start | bytes 3145736 | tf_op jit(solution)/shard_map/ppermute | solution.py:325
  197.0 63.2 %copy-start.5 = (f32[16,128,128]{2,1,0:T(8,128)S(1)}, f32[16,128,128]{2,1,0:T(8,128)}, u32[]{:S(2)}) copy-start(f32[16,128,128]{2,1,0:T(8,128)} %copy-done.4) | copy-start | bytes 3145732
  197.1 63.3 %copy-start.10 = (f32[16]{0:T(128)S(1)}, f32[16]{0:T(128)}, u32[]{:S(2)}) copy-start(f32[16]{0:T(128)} %param.5) | copy-start | bytes 196
  257.5 8.0 %collective-permute-start.13 = (f32[16,128,128]{2,1,0:T(8,128)}, f32[16,128,128]{2,1,0:T(8,128)}, u32[]{:S(2)}, u32[]{:S(2)}) collective-permute-start(f32[16,128,128]{2,1,0:T(8,128)} %collective-permute-done.refs_0_), channel_id=1, source_target_pairs={{0,8},{1,9},{2,10},{3,11},{4,12},{5,13},{6,14},{7,15},{8,0},{9,1},... | collective-permute-start | bytes 3145736 | tf_op jit(solution)/shard_map/ppermute | solution.py:325
  257.5 9.3 %collective-permute-start.15 = (f32[16,128,128]{2,1,0:T(8,128)S(1)}, f32[16,128,128]{2,1,0:T(8,128)}, u32[]{:S(2)}, u32[]{:S(2)}) collective-permute-start(f32[16,128,128]{2,1,0:T(8,128)S(1)} %broadcast_select_fusion.3.refs_2_), channel_id=1, source_target_pairs={{0,8},{1,9},{2,10},{3,11},{4,12},{5,13},{6,14},{7,15},{8,0},{9,1},... | collective-permute-start | bytes 3145736 | tf_op jit(solution)/shard_map/ppermute | solution.py:325
  258.0 24.9 %collective-permute-start.24 = (f32[2,8,128,128]{3,2,1,0:T(8,128)}, f32[2,8,128,128]{3,2,1,0:T(8,128)}, u32[]{:S(2)}, u32[]{:S(2)}) collective-permute-start(f32[2,8,128,128]{3,2,1,0:T(8,128)} %slice.152), channel_id=1, source_target_pairs={{0,1},{1,0},{2,3},{3,2},{4,5},{5,4},{6,7},{7,6},{8,9},{9,8},{10,11... | collective-permute-start | bytes 3145736 | tf_op jit(solution)/shard_map/ppermute | solution.py:325
  259.5 24.6 %collective-permute-start.16 = (f32[16,128,128]{2,1,0:T(8,128)S(1)}, f32[16,128,128]{2,1,0:T(8,128)}, u32[]{:S(2)}, u32[]{:S(2)}) collective-permute-start(f32[16,128,128]{2,1,0:T(8,128)S(1)} %broadcast_select_fusion.1.refs_3_), channel_id=1, source_target_pairs={{0,8},{1,9},{2,10},{3,11},{4,12},{5,13},{6,14},{7,15},{8,0},{9,1},... | collective-permute-start | bytes 3145736 | tf_op jit(solution)/shard_map/ppermute | solution.py:325
  260.3 25.7 %collective-permute-start.14 = (f32[16,128,128]{2,1,0:T(8,128)S(1)}, f32[16,128,128]{2,1,0:T(8,128)}, u32[]{:S(2)}, u32[]{:S(2)}) collective-permute-start(f32[16,128,128]{2,1,0:T(8,128)S(1)} %broadcast_select_fusion.5.refs_1_), channel_id=1, source_target_pairs={{0,8},{1,9},{2,10},{3,11},{4,12},{5,13},{6,14},{7,15},{8,0},{9,1},... | collective-permute-start | bytes 3145736 | tf_op jit(solution)/shard_map/ppermute | solution.py:325
  265.5 54.7 %collective-permute-start.26 = (f32[2,8,128,128]{3,2,1,0:T(8,128)S(1)}, f32[2,8,128,128]{3,2,1,0:T(8,128)S(1)}, u32[]{:S(2)}, u32[]{:S(2)}) collective-permute-start(f32[2,8,128,128]{3,2,1,0:T(8,128)S(1)} %slice.153), channel_id=1, source_target_pairs={{0,16},{1,17},{2,18},{3,19},{4,20},{5,21},{6,22},{7,23},{8,24},{9,... | collective-permute-start | bytes 3145736 | tf_op jit(solution)/shard_map/ppermute | solution.py:325
  266.7 53.5 %collective-permute-start.28 = (f32[2,8,128,128]{3,2,1,0:T(8,128)S(1)}, f32[2,8,128,128]{3,2,1,0:T(8,128)}, u32[]{:S(2)}, u32[]{:S(2)}) collective-permute-start(f32[2,8,128,128]{3,2,1,0:T(8,128)S(1)} %slice.154), channel_id=1, source_target_pairs={{0,1},{1,0},{2,3},{3,2},{4,5},{5,4},{6,7},{7,6},{8,9},{9,8},{10,11... | collective-permute-start | bytes 3145736 | tf_op jit(solution)/shard_map/ppermute | solution.py:325
  282.9 37.3 %collective-permute-start.30 = (f32[2,8,128,128]{3,2,1,0:T(8,128)S(1)}, f32[2,8,128,128]{3,2,1,0:T(8,128)}, u32[]{:S(2)}, u32[]{:S(2)}) collective-permute-start(f32[2,8,128,128]{3,2,1,0:T(8,128)S(1)} %slice.155), channel_id=1, source_target_pairs={{0,16},{1,17},{2,18},{3,19},{4,20},{5,21},{6,22},{7,23},{8,24},{9,... | collective-permute-start | bytes 3145736 | tf_op jit(solution)/shard_map/ppermute | solution.py:325
  284.1 30.7 %collective-permute-start.42 = (f32[16,128,128]{2,1,0:T(8,128)S(1)}, f32[16,128,128]{2,1,0:T(8,128)S(1)}, u32[]{:S(2)}, u32[]{:S(2)}) collective-permute-start(f32[16,128,128]{2,1,0:T(8,128)S(1)} %copy-done.1), channel_id=1, source_target_pairs={{0,2},{1,3},{2,4},{3,5},{4,6},{5,7},{8,10},{9,11},{10,12},{11,13},... | collective-permute-start | bytes 3145736 | tf_op jit(solution)/shard_map/ppermute | solution.py:325
  286.0 30.7 %collective-permute-start.41 = (f32[16,128,128]{2,1,0:T(8,128)S(1)}, f32[16,128,128]{2,1,0:T(8,128)S(1)}, u32[]{:S(2)}, u32[]{:S(2)}) collective-permute-start(f32[16,128,128]{2,1,0:T(8,128)S(1)} %copy-done.1), channel_id=1, source_target_pairs={{2,0},{3,1},{4,2},{5,3},{6,4},{7,5},{10,8},{11,9},{12,10},{13,11},... | collective-permute-start | bytes 3145736 | tf_op jit(solution)/shard_map/ppermute | solution.py:325
  314.8 34.2 %collective-permute-start.43 = (f32[16,128,128]{2,1,0:T(8,128)S(1)}, f32[16,128,128]{2,1,0:T(8,128)S(1)}, u32[]{:S(2)}, u32[]{:S(2)}) collective-permute-start(f32[16,128,128]{2,1,0:T(8,128)S(1)} %collective-permute-done.42), channel_id=1, source_target_pairs={{2,4},{3,5},{4,6},{5,7},{10,12},{11,13},{12,14},{13,15},{18,20},{1... | collective-permute-start | bytes 3145736 | tf_op jit(solution)/shard_map/ppermute | solution.py:325
  316.7 33.7 %collective-permute-start.45 = (f32[16,128,128]{2,1,0:T(8,128)S(1)}, f32[16,128,128]{2,1,0:T(8,128)S(1)}, u32[]{:S(2)}, u32[]{:S(2)}) collective-permute-start(f32[16,128,128]{2,1,0:T(8,128)S(1)} %collective-permute-done.41), channel_id=1, source_target_pairs={{2,0},{3,1},{4,2},{5,3},{10,8},{11,9},{12,10},{13,11},{18,16},{19,... | collective-permute-start | bytes 3145736 | tf_op jit(solution)/shard_map/ppermute | solution.py:325
  346.2 27.8 %collective-permute-start.31 = (f32[2,16,128,128]{3,2,1,0:T(8,128)}, f32[2,16,128,128]{3,2,1,0:T(8,128)S(1)}, u32[]{:S(2)}, u32[]{:S(2)}) collective-permute-start(f32[2,16,128,128]{3,2,1,0:T(8,128)} %get-tuple-element.32), channel_id=1, source_target_pairs={{0,8},{1,9},{2,10},{3,11},{4,12},{5,13},{6,14},{7,15},{8,0},{9,1},... | collective-permute-start | bytes 6291464 | tf_op jit(solution)/shard_map/ppermute | solution.py:325
  349.0 24.0 %collective-permute-start.44 = (f32[16,128,128]{2,1,0:T(8,128)S(1)}, f32[16,128,128]{2,1,0:T(8,128)S(1)}, u32[]{:S(2)}, u32[]{:S(2)}) collective-permute-start(f32[16,128,128]{2,1,0:T(8,128)S(1)} %collective-permute-done.43), channel_id=1, source_target_pairs={{4,6},{5,7},{12,14},{13,15},{20,22},{21,23},{28,30},{29,31}} | collective-permute-start | bytes 3145736 | tf_op jit(solution)/shard_map/ppermute | solution.py:325
  350.3 24.2 %collective-permute-start.32 = (f32[2,16,128,128]{3,2,1,0:T(8,128)}, f32[2,16,128,128]{3,2,1,0:T(8,128)S(1)}, u32[]{:S(2)}, u32[]{:S(2)}) collective-permute-start(f32[2,16,128,128]{3,2,1,0:T(8,128)} %get-tuple-element.34), channel_id=1, source_target_pairs={{0,8},{1,9},{2,10},{3,11},{4,12},{5,13},{6,14},{7,15},{8,0},{9,1},... | collective-permute-start | bytes 6291464 | tf_op jit(solution)/shard_map/ppermute | solution.py:325
  350.4 23.3 %collective-permute-start.46 = (f32[16,128,128]{2,1,0:T(8,128)S(1)}, f32[16,128,128]{2,1,0:T(8,128)S(1)}, u32[]{:S(2)}, u32[]{:S(2)}) collective-permute-start(f32[16,128,128]{2,1,0:T(8,128)S(1)} %collective-permute-done.45), channel_id=1, source_target_pairs={{2,0},{3,1},{10,8},{11,9},{18,16},{19,17},{26,24},{27,25}} | collective-permute-start | bytes 3145736 | tf_op jit(solution)/shard_map/ppermute | solution.py:325
  351.3 26.5 %collective-permute-start.47 = (f32[16,128,128]{2,1,0:T(8,128)S(1)}, f32[16,128,128]{2,1,0:T(8,128)S(1)}, u32[]{:S(2)}, u32[]{:S(2)}) collective-permute-start(f32[16,128,128]{2,1,0:T(8,128)S(1)} %copy-done.1), channel_id=1, source_target_pairs={{0,8},{1,9},{2,10},{3,11},{4,12},{5,13},{6,14},{7,15},{8,0},{9,1},... | collective-permute-start | bytes 3145736 | tf_op jit(solution)/shard_map/ppermute | solution.py:325
  373.0 5.6 collective-permute-start.49
  373.8 4.9 collective-permute-start.48
  374.0 4.9 collective-permute-start.50
  376.6 28.9 %collective-permute-start.33 = (f32[16,128,128]{2,1,0:T(8,128)S(1)}, f32[16,128,128]{2,1,0:T(8,128)S(1)}, u32[]{:S(2)}, u32[]{:S(2)}) collective-permute-start(f32[16,128,128]{2,1,0:T(8,128)S(1)} %get-tuple-element.38), channel_id=1, source_target_pairs={{6,4},{7,5},{14,12},{15,13},{22,20},{23,21},{30,28},{31,29}} | collective-permute-start | bytes 3145736 | tf_op jit(solution)/shard_map/ppermute | solution.py:325
  377.9 27.6 %collective-permute-start.34 = (f32[16,128,128]{2,1,0:T(8,128)S(1)}, f32[16,128,128]{2,1,0:T(8,128)S(1)}, u32[]{:S(2)}, u32[]{:S(2)}) collective-permute-start(f32[16,128,128]{2,1,0:T(8,128)S(1)} %get-tuple-element.39), channel_id=1, source_target_pairs={{0,2},{1,3},{8,10},{9,11},{16,18},{17,19},{24,26},{25,27}} | collective-permute-start | bytes 3145736 | tf_op jit(solution)/shard_map/ppermute | solution.py:325
  430.2 4.4 collective-permute-start.51
  430.3 7.4 %collective-permute-start.52 = (f32[2,16,128,128]{3,2,1,0:T(8,128)}, f32[2,16,128,128]{3,2,1,0:T(8,128)S(1)}, u32[]{:S(2)}, u32[]{:S(2)}) collective-permute-start(f32[2,16,128,128]{3,2,1,0:T(8,128)} %get-tuple-element.49), channel_id=1, source_target_pairs={{0,8},{1,9},{2,10},{3,11},{4,12},{5,13},{6,14},{7,15},{8,0},{9,1},... | collective-permute-start | bytes 6291464 | tf_op jit(solution)/shard_map/ppermute | solution.py:325
  440.6 26.8 %collective-permute-start.53 = (f32[16,128,128]{2,1,0:T(8,128)S(1)}, f32[16,128,128]{2,1,0:T(8,128)S(1)}, u32[]{:S(2)}, u32[]{:S(2)}) collective-permute-start(f32[16,128,128]{2,1,0:T(8,128)S(1)} %get-tuple-element.52), channel_id=1, source_target_pairs={{6,4},{7,5},{14,12},{15,13},{22,20},{23,21},{30,28},{31,29}} | collective-permute-start | bytes 3145736 | tf_op jit(solution)/shard_map/ppermute | solution.py:325
  441.9 25.6 %collective-permute-start.56 = (f32[16,128,128]{2,1,0:T(8,128)S(1)}, f32[16,128,128]{2,1,0:T(8,128)S(1)}, u32[]{:S(2)}, u32[]{:S(2)}) collective-permute-start(f32[16,128,128]{2,1,0:T(8,128)S(1)} %get-tuple-element.50), channel_id=1, source_target_pairs={{0,2},{1,3},{8,10},{9,11},{16,18},{17,19},{24,26},{25,27}} | collective-permute-start | bytes 3145736 | tf_op jit(solution)/shard_map/ppermute | solution.py:325
  442.6 47.3 %collective-permute-start.35 = (f32[16,128,128]{2,1,0:T(8,128)S(1)}, f32[16,128,128]{2,1,0:T(8,128)S(1)}, u32[]{:S(2)}, u32[]{:S(2)}) collective-permute-start(f32[16,128,128]{2,1,0:T(8,128)S(1)} %get-tuple-element.40), channel_id=1, source_target_pairs={{4,2},{5,3},{6,4},{7,5},{12,10},{13,11},{14,12},{15,13},{20,18},{2... | collective-permute-start | bytes 3145736 | tf_op jit(solution)/shard_map/ppermute | solution.py:325
  444.6 47.4 %collective-permute-start.37 = (f32[16,128,128]{2,1,0:T(8,128)S(1)}, f32[16,128,128]{2,1,0:T(8,128)S(1)}, u32[]{:S(2)}, u32[]{:S(2)}) collective-permute-start(f32[16,128,128]{2,1,0:T(8,128)S(1)} %get-tuple-element.41), channel_id=1, source_target_pairs={{0,2},{1,3},{2,4},{3,5},{8,10},{9,11},{10,12},{11,13},{16,18},{17,... | collective-permute-start | bytes 3145736 | tf_op jit(solution)/shard_map/ppermute | solution.py:325
  467.6 44.7 %collective-permute-start.54 = (f32[16,128,128]{2,1,0:T(8,128)S(1)}, f32[16,128,128]{2,1,0:T(8,128)S(1)}, u32[]{:S(2)}, u32[]{:S(2)}) collective-permute-start(f32[16,128,128]{2,1,0:T(8,128)S(1)} %get-tuple-element.81), channel_id=1, source_target_pairs={{4,2},{5,3},{6,4},{7,5},{12,10},{13,11},{14,12},{15,13},{20,18},{2... | collective-permute-start | bytes 3145736 | tf_op jit(solution)/shard_map/ppermute | solution.py:325
  469.6 44.9 %collective-permute-start.57 = (f32[16,128,128]{2,1,0:T(8,128)S(1)}, f32[16,128,128]{2,1,0:T(8,128)S(1)}, u32[]{:S(2)}, u32[]{:S(2)}) collective-permute-start(f32[16,128,128]{2,1,0:T(8,128)S(1)} %get-tuple-element.82), channel_id=1, source_target_pairs={{0,2},{1,3},{2,4},{3,5},{8,10},{9,11},{10,12},{11,13},{16,18},{17,... | collective-permute-start | bytes 3145736 | tf_op jit(solution)/shard_map/ppermute | solution.py:325
  490.0 44.8 %collective-permute-start.36 = (f32[16,128,128]{2,1,0:T(8,128)S(1)}, f32[16,128,128]{2,1,0:T(8,128)S(1)}, u32[]{:S(2)}, u32[]{:S(2)}) collective-permute-start(f32[16,128,128]{2,1,0:T(8,128)S(1)} %add.225), channel_id=1, source_target_pairs={{2,0},{3,1},{4,2},{5,3},{6,4},{7,5},{10,8},{11,9},{12,10},{13,11},... | collective-permute-start | bytes 3145736 | tf_op jit(solution)/shard_map/ppermute | solution.py:325
  492.1 42.8 %collective-permute-start.38 = (f32[16,128,128]{2,1,0:T(8,128)S(1)}, f32[16,128,128]{2,1,0:T(8,128)S(1)}, u32[]{:S(2)}, u32[]{:S(2)}) collective-permute-start(f32[16,128,128]{2,1,0:T(8,128)S(1)} %add.227), channel_id=1, source_target_pairs={{0,2},{1,3},{2,4},{3,5},{4,6},{5,7},{8,10},{9,11},{10,12},{11,13},... | collective-permute-start | bytes 3145736 | tf_op jit(solution)/shard_map/ppermute | solution.py:325
  512.5 44.8 %collective-permute-start.55 = (f32[16,128,128]{2,1,0:T(8,128)S(1)}, f32[16,128,128]{2,1,0:T(8,128)S(1)}, u32[]{:S(2)}, u32[]{:S(2)}) collective-permute-start(f32[16,128,128]{2,1,0:T(8,128)S(1)} %add.238), channel_id=1, source_target_pairs={{2,0},{3,1},{4,2},{5,3},{6,4},{7,5},{10,8},{11,9},{12,10},{13,11},... | collective-permute-start | bytes 3145736 | tf_op jit(solution)/shard_map/ppermute | solution.py:325
  514.6 42.8 %collective-permute-start.58 = (f32[16,128,128]{2,1,0:T(8,128)S(1)}, f32[16,128,128]{2,1,0:T(8,128)S(1)}, u32[]{:S(2)}, u32[]{:S(2)}) collective-permute-start(f32[16,128,128]{2,1,0:T(8,128)S(1)} %add.241), channel_id=1, source_target_pairs={{0,2},{1,3},{2,4},{3,5},{4,6},{5,7},{8,10},{9,11},{10,12},{11,13},... | collective-permute-start | bytes 3145736 | tf_op jit(solution)/shard_map/ppermute | solution.py:325
  535.1 26.8 %collective-permute-start.39 = (f32[16,128,128]{2,1,0:T(8,128)S(1)}, f32[16,128,128]{2,1,0:T(8,128)S(1)}, u32[]{:S(2)}, u32[]{:S(2)}) collective-permute-start(f32[16,128,128]{2,1,0:T(8,128)S(1)} %add_add_fusion.1), channel_id=1, source_target_pairs={{0,0},{1,8},{2,2},{3,10},{4,4},{5,12},{6,6},{7,14},{8,1},{9,9},{10... | collective-permute-start | bytes 3145736 | tf_op jit(solution)/shard_map/ppermute | solution.py:325
  557.5 16.8 %collective-permute-start.59 = (f32[16,128,128]{2,1,0:T(8,128)S(1)}, f32[16,128,128]{2,1,0:T(8,128)S(1)}, u32[]{:S(2)}, u32[]{:S(2)}) collective-permute-start(f32[16,128,128]{2,1,0:T(8,128)S(1)} %add_add_fusion), channel_id=1, source_target_pairs={{0,0},{1,8},{2,2},{3,10},{4,4},{5,12},{6,6},{7,14},{8,1},{9,9},{10... | collective-permute-start | bytes 3145736 | tf_op jit(solution)/shard_map/ppermute | solution.py:325
  (11 other events, 39.6 us)
where the time goes:
time: 577 us; the launch traced here: 576 us
  waiting for transfers between devices  354 us (61%)
  Pallas kernels  98.8 us (17%)
  starting transfers between devices  90.2 us (16%)
  local copies, waits for them, and re-layouts  17.2 us (3%)
  other arithmetic  15.1 us (3%)
    ppermute x60, waiting for transfers between devices, send(): return lax.ppermute(value, names, pairs)  354 us
    pallas_call x4, Pallas kernels, exchange(): pl.pallas_call(functools.partial(exchange_kernel, n, slots, layout, last)...  98.8 us
    ppermute x60, starting transfers between devices, send(): return lax.ppermute(value, names, pairs)  90.2 us
  transfers between devices with their start and end apart: 60, of which 23 were waited for; matrix products, arithmetic and copies ran while one was open for 3% of the time, Pallas kernels for 13%

commit v1 on v0

--- a/solution.py
+++ b/solution.py
@@ -138,7 +138,7 @@
     return jnp.concatenate([cols[:, k * size : (k + 1) * size] for k in range(count)], 0)
 
 
-STEP = 16
+STEP = 32
 PAD = 8
 PARTS = 2
 
@@ -290,7 +290,7 @@
         scratch_shapes=[
             pltpu.VMEM((n, n, n), F32),
             pltpu.VMEM((n, n, n), F32),
-            pltpu.VMEM((n * (n + PAD), n), F32),
+            pltpu.VMEM((n * (n + PAD) + n, n), F32),
             pltpu.VMEM((n, n, n), F32),
             pltpu.SemaphoreType.DMA((2, slots)),
             pltpu.SemaphoreType.DMA((slots, 2, PARTS)),
@@ -429,7 +429,7 @@
         and lax.axis_size("slab") == 8
         and resident.shape[0] == 2
         and blocks.shape[0] == 4
-        and resident.shape[1] % STEP == 0
+        and 2 * resident.shape[1] % STEP == 0
     ):
         return whole_grids(resident, blocks, occupation)
     return sliced_grids(resident, blocks, occupation)

time: 577 us -> 568 us (0.984)
  Pallas kernels: 98.8 us -> 89.8 us
    pallas_call x4, Pallas kernels: 98.8 us -> 89.8 us  [exchange(): pl.pallas_call(functools.partial(exchange_kernel, n, slots, layout, last)...]
  transfers between devices with their start and end apart: 60 -> 60, of which waited for: 23 -> 23; matrix products, arithmetic and copies ran while one was open for 3% -> 3% of each run, Pallas kernels for 13% -> 12%
where the time goes in v1:
time: 568 us; the launch traced here: 567 us
  waiting for transfers between devices  352 us (62%)
  starting transfers between devices  92 us (16%)
  Pallas kernels  89.8 us (16%)
  local copies, waits for them, and re-layouts  17.4 us (3%)
  other arithmetic  15.1 us (3%)
    ppermute x60, waiting for transfers between devices, send(): return lax.ppermute(value, names, pairs)  352 us
    ppermute x60, starting transfers between devices, send(): return lax.ppermute(value, names, pairs)  92 us
    pallas_call x4, Pallas kernels, exchange(): pl.pallas_call(functools.partial(exchange_kernel, n, slots, layout, last)...  89.8 us
  transfers between devices with their start and end apart: 60, of which 23 were waited for; matrix products, arithmetic and copies ran while one was open for 3% of the time, Pallas kernels for 12%

profile of v1, /device:TPU:17, one launch (start us, length us, event | category | flops | bytes accessed | tf_op | source)
XLA Modules:
  0.0 567.3 jit_solution(11546689321002089622)
XLA Ops:
  0.0 3.3 dynamic-slice_bitcast_fusion.1
  3.3 1.8 collective-permute-start.17
  6.5 3.2 collective-permute-start
  9.7 1.6 collective-permute-start.3
  11.3 6.5 %collective-permute-done.17 = f32[8,128,128]{2,1,0:T(8,128)} collective-permute-done((f32[8,128,128]{2,1,0:T(8,128)S(1)}, f32[8,128,128]{2,1,0:T(8,128)}, u32[]{:S(2)}, u32[]{:S(2)}) %collective-permute-start.17) | collective-permute-done | bytes 524320 | tf_op jit(solution)/shard_map/ppermute | solution.py:325
  19.1 10.0 %collective-permute-done.18 = f32[8,128,128]{2,1,0:T(8,128)} collective-permute-done((f32[8,128,128]{2,1,0:T(8,128)S(1)}, f32[8,128,128]{2,1,0:T(8,128)}, u32[]{:S(2)}, u32[]{:S(2)}) %collective-permute-start.18) | collective-permute-done | bytes 524320 | tf_op jit(solution)/shard_map/ppermute | solution.py:325
  29.5 1.8 select_bitcast_fusion
  31.6 8.7 %collective-permute-done.3 = f32[8,128,128]{2,1,0:T(8,128)S(1)} collective-permute-done((f32[8,128,128]{2,1,0:T(8,128)}, f32[8,128,128]{2,1,0:T(8,128)S(1)}, u32[]{:S(2)}, u32[]{:S(2)}) %collective-permute-start.3) | collective-permute-done | bytes 524320 | tf_op jit(solution)/shard_map/ppermute | solution.py:325
  40.3 11.1 %collective-permute-done.4 = f32[8,128,128]{2,1,0:T(8,128)S(1)} collective-permute-done((f32[8,128,128]{2,1,0:T(8,128)S(1)}, f32[8,128,128]{2,1,0:T(8,128)S(1)}, u32[]{:S(2)}, u32[]{:S(2)}) %collective-permute-start.4) | collective-permute-done | bytes 524320 | tf_op jit(solution)/shard_map/ppermute | solution.py:325
  51.4 1.3 collective-permute-start.22
  52.7 2.1 collective-permute-start.1
  54.8 3.3 collective-permute-start.2
  58.1 1.5 select_bitcast_fusion.1
  59.6 16.9 %collective-permute-done.21 = f32[8,128,128]{2,1,0:T(8,128)S(1)} collective-permute-done((f32[8,128,128]{2,1,0:T(8,128)S(1)}, f32[8,128,128]{2,1,0:T(8,128)S(1)}, u32[]{:S(2)}, u32[]{:S(2)}) %collective-permute-start.21) | collective-permute-done | bytes 524320 | tf_op jit(solution)/shard_map/ppermute | solution.py:325
  76.6 4.4 collective-permute-done.22
  80.9 1.5 pad_maximum_fusion.1.refs_8_
  82.4 54.7 %collective-permute-done.8 = f32[8,128,128]{2,1,0:T(8,128)S(1)} collective-permute-done((f32[8,128,128]{2,1,0:T(8,128)S(1)}, f32[8,128,128]{2,1,0:T(8,128)S(1)}, u32[]{:S(2)}, u32[]{:S(2)}) %collective-permute-start.8) | collective-permute-done | bytes 524320 | tf_op jit(solution)/shard_map/ppermute | solution.py:325
  138.3 5.7 %collective-permute-done.7 = f32[8,128,128]{2,1,0:T(8,128)S(1)} collective-permute-done((f32[8,128,128]{2,1,0:T(8,128)S(1)}, f32[8,128,128]{2,1,0:T(8,128)S(1)}, u32[]{:S(2)}, u32[]{:S(2)}) %collective-permute-start.7) | collective-permute-done | bytes 524320 | tf_op jit(solution)/shard_map/ppermute | solution.py:325
  144.0 1.4 pad_maximum_fusion.refs_10_
  145.5 5.6 collective-permute-start.11
  151.1 2.6 collective-permute-start.9
  153.6 1.3 collective-permute-start.25
  155.2 17.8 %collective-permute-done.11 = f32[16,128,128]{2,1,0:T(8,128)S(1)} collective-permute-done((f32[16,128,128]{2,1,0:T(8,128)S(1)}, f32[16,128,128]{2,1,0:T(8,128)S(1)}, u32[]{:S(2)}, u32[]{:S(2)}) %collective-permute-start.11) | collective-permute-done | bytes 1048608 | tf_op jit(solution)/shard_map/ppermute | solution.py:325
  173.7 3.3 collective-permute-done.9
  178.2 5.9 %collective-permute-done.23.refs_8_ = f32[4,8,128,128]{3,2,1,0:T(8,128)} collective-permute-done((f32[4,8,128,128]{3,2,1,0:T(8,128)}, f32[4,8,128,128]{3,2,1,0:T(8,128)}, u32[]{:S(2)}, u32[]{:S(2)}) %collective-permute-start.23) | collective-permute-done | bytes 2097184 | tf_op jit(solution)/shard_map/ppermute | solution.py:325
  184.1 5.4 collective-permute-start.40
  190.5 2.3 collective-permute-start.10
  192.8 2.3 slice.152
  195.2 1.5 broadcast_select_fusion.3.refs_2_
  197.2 60.3 %collective-permute-done.40.refs_0_ = f32[16,128,128]{2,1,0:T(8,128)S(1)} collective-permute-done((f32[16,128,128]{2,1,0:T(8,128)}, f32[16,128,128]{2,1,0:T(8,128)S(1)}, u32[]{:S(2)}, u32[]{:S(2)}) %collective-permute-start.40) | collective-permute-done | bytes 1048608 | tf_op jit(solution)/shard_map/ppermute | solution.py:325
  258.0 1.5 collective-permute-start.24
  261.5 1.3 slice.153
  262.8 1.4 slice.154
  264.2 1.3 slice.155
  266.9 15.9 %collective-permute-done.24.refs_9_ = f32[2,8,128,128]{3,2,1,0:T(8,128)} collective-permute-done((f32[2,8,128,128]{3,2,1,0:T(8,128)}, f32[2,8,128,128]{3,2,1,0:T(8,128)}, u32[]{:S(2)}, u32[]{:S(2)}) %collective-permute-start.24) | collective-permute-done | bytes 1048608 | tf_op jit(solution)/shard_map/ppermute | solution.py:325
  284.1 1.9 collective-permute-start.42
  286.0 3.7 collective-permute-start.41
  289.8 22.6 %exchange.4.refs_14_ = f32[128,128,128]{2,1,0:T(8,128)} custom-call(s32[2]{0:T(128)S(1)} %pad_add_fusion.where_ref, f32[1]{0:T(128)} %get-tuple-element.87.occ_ref, f32[1,128]{1,0:T(1,128)S(1)} %fusion.21.gx_ref, f32[128,128]{1,0:T(8,128)S(1)} %broadcast_in_dim.8.gz_ref, bf16[256,256]{1,0:T(8,128)(2,1)S(1)} %get-tuple-element.86.right_ref, ...), custom_call_target="tpu_custom_call" | custom-call | flops 19327352832 | bytes 25165824 | tf_op jit(solution)/shard_map/exchange/pallas_call | solution.py:285
  312.4 1.9 collective-permute-start.43
  314.3 3.7 collective-permute-start.45
  319.0 22.7 %exchange.5 = (f32[4,16,128,128]{3,2,1,0:T(8,128)}, f32[2,16,128,128]{3,2,1,0:T(8,128)}, f32[2,16,128,128]{3,2,1,0:T(8,128)}) custom-call(s32[2]{0:T(128)S(1)} %pad_add_fusion.where_ref, f32[1]{0:T(128)} %get-tuple-element.88.occ_ref, f32[1,128]{1,0:T(1,128)S(1)} %fusion.21.gx_ref, f32[128,128]{1,0:T(8,128)S(1)} %broadcast_in_dim.8.gz_ref, ...), custom_call_target="tpu_custom_call" | custom-call | flops 19327352832 | bytes 41943040 | tf_op jit(solution)/shard_map/exchange/pallas_call | solution.py:285
  341.8 2.8 collective-permute-start.31
  344.6 1.3 collective-permute-start.44
  347.5 21.2 %collective-permute-done.44 = f32[16,128,128]{2,1,0:T(8,128)S(1)} collective-permute-done((f32[16,128,128]{2,1,0:T(8,128)S(1)}, f32[16,128,128]{2,1,0:T(8,128)S(1)}, u32[]{:S(2)}, u32[]{:S(2)}) %collective-permute-start.44) | collective-permute-done | bytes 1048608 | tf_op jit(solution)/shard_map/ppermute | solution.py:325
  376.8 22.1 %exchange.6.refs_14_ = f32[128,128,128]{2,1,0:T(8,128)} custom-call(s32[2]{0:T(128)S(1)} %pad_add_fusion.where_ref, f32[1]{0:T(128)} %get-tuple-element.87.occ_ref, f32[1,128]{1,0:T(1,128)S(1)} %fusion.21.gx_ref, f32[128,128]{1,0:T(8,128)S(1)} %broadcast_in_dim.8.gz_ref, bf16[256,256]{1,0:T(8,128)(2,1)S(1)} %get-tuple-element.86.right_ref, ...), custom_call_target="tpu_custom_call" | custom-call | flops 19327352832 | bytes 25165824 | tf_op jit(solution)/shard_map/exchange/pallas_call | solution.py:285
  399.3 22.3 %exchange.7 = (f32[4,16,128,128]{3,2,1,0:T(8,128)}, f32[2,16,128,128]{3,2,1,0:T(8,128)}, f32[2,16,128,128]{3,2,1,0:T(8,128)}) custom-call(s32[2]{0:T(128)S(1)} %pad_add_fusion.where_ref, f32[1]{0:T(128)} %get-tuple-element.88.occ_ref, f32[1,128]{1,0:T(1,128)S(1)} %fusion.21.gx_ref, f32[128,128]{1,0:T(8,128)S(1)} %broadcast_in_dim.8.gz_ref, ...), custom_call_target="tpu_custom_call" | custom-call | flops 19327352832 | bytes 41943040 | tf_op jit(solution)/shard_map/exchange/pallas_call | solution.py:285
  422.5 3.9 collective-permute-done.51
  426.4 3.0 collective-permute-done.52
  429.4 2.9 fusion.2
  434.4 1.9 collective-permute-start.35
  437.6 21.0 %collective-permute-done.53 = f32[16,128,128]{2,1,0:T(8,128)S(1)} collective-permute-done((f32[16,128,128]{2,1,0:T(8,128)S(1)}, f32[16,128,128]{2,1,0:T(8,128)S(1)}, u32[]{:S(2)}, u32[]{:S(2)}) %collective-permute-start.53) | collective-permute-done | bytes 1048608 | tf_op jit(solution)/shard_map/ppermute | solution.py:325
  458.8 1.9 collective-permute-start.54
  462.0 19.0 %collective-permute-done.35 = f32[16,128,128]{2,1,0:T(8,128)S(1)} collective-permute-done((f32[16,128,128]{2,1,0:T(8,128)S(1)}, f32[16,128,128]{2,1,0:T(8,128)S(1)}, u32[]{:S(2)}, u32[]{:S(2)}) %collective-permute-start.35) | collective-permute-done | bytes 1048608 | tf_op jit(solution)/shard_map/ppermute | solution.py:325
  481.2 1.9 collective-permute-start.36
  483.2 3.4 collective-permute-start.38
  486.7 16.8 %collective-permute-done.54 = f32[16,128,128]{2,1,0:T(8,128)S(1)} collective-permute-done((f32[16,128,128]{2,1,0:T(8,128)S(1)}, f32[16,128,128]{2,1,0:T(8,128)S(1)}, u32[]{:S(2)}, u32[]{:S(2)}) %collective-permute-start.54) | collective-permute-done | bytes 1048608 | tf_op jit(solution)/shard_map/ppermute | solution.py:325
  503.6 1.9 collective-permute-start.55
  505.7 3.4 collective-permute-start.58
  509.1 16.9 %collective-permute-done.36 = f32[16,128,128]{2,1,0:T(8,128)S(1)} collective-permute-done((f32[16,128,128]{2,1,0:T(8,128)S(1)}, f32[16,128,128]{2,1,0:T(8,128)S(1)}, u32[]{:S(2)}, u32[]{:S(2)}) %collective-permute-start.36) | collective-permute-done | bytes 1048608 | tf_op jit(solution)/shard_map/ppermute | solution.py:325
  526.2 5.6 collective-permute-start.39
  531.8 16.6 %collective-permute-done.55 = f32[16,128,128]{2,1,0:T(8,128)S(1)} collective-permute-done((f32[16,128,128]{2,1,0:T(8,128)S(1)}, f32[16,128,128]{2,1,0:T(8,128)S(1)}, u32[]{:S(2)}, u32[]{:S(2)}) %collective-permute-start.55) | collective-permute-done | bytes 1048608 | tf_op jit(solution)/shard_map/ppermute | solution.py:325
  548.6 4.8 collective-permute-start.59
  553.4 12.5 %collective-permute-done.59 = f32[16,128,128]{2,1,0:T(8,128)S(1)} collective-permute-done((f32[16,128,128]{2,1,0:T(8,128)S(1)}, f32[16,128,128]{2,1,0:T(8,128)S(1)}, u32[]{:S(2)}, u32[]{:S(2)}) %collective-permute-start.59) | collective-permute-done | bytes 1048608 | tf_op jit(solution)/shard_map/ppermute | solution.py:325
  565.9 1.5 pad_maximum_fusion.2
  (124 shorter events, 31.0 us)
Async XLA Ops:
  3.3 14.6 %collective-permute-start.17 = (f32[8,128,128]{2,1,0:T(8,128)S(1)}, f32[8,128,128]{2,1,0:T(8,128)}, u32[]{:S(2)}, u32[]{:S(2)}) collective-permute-start(f32[8,128,128]{2,1,0:T(8,128)S(1)} %get-tuple-element.78), channel_id=1, source_target_pairs={{0,24},{1,25},{2,26},{3,27},{4,28},{5,29},{6,30},{7,31},{8,16},{9,... | collective-permute-start | bytes 1572872 | tf_op jit(solution)/shard_map/ppermute | solution.py:325
  5.0 24.0 %collective-permute-start.18 = (f32[8,128,128]{2,1,0:T(8,128)S(1)}, f32[8,128,128]{2,1,0:T(8,128)}, u32[]{:S(2)}, u32[]{:S(2)}) collective-permute-start(f32[8,128,128]{2,1,0:T(8,128)S(1)} %get-tuple-element.77), channel_id=1, source_target_pairs={{0,16},{1,17},{2,18},{3,19},{4,20},{5,21},{6,22},{7,23},{8,24},{9,... | collective-permute-start | bytes 1572872 | tf_op jit(solution)/shard_map/ppermute | solution.py:325
  6.5 46.2 %collective-permute-start = (f32[16,128,128]{2,1,0:T(8,128)S(1)}, f32[16,128,128]{2,1,0:T(8,128)}, u32[]{:S(2)}, u32[]{:S(2)}) collective-permute-start(f32[16,128,128]{2,1,0:T(8,128)S(1)} %get-tuple-element.80), channel_id=1, source_target_pairs={{0,0},{1,8},{2,2},{3,10},{4,4},{5,12},{6,6},{7,14},{8,1},{9,9},{10... | collective-permute-start | bytes 3145736 | tf_op jit(solution)/shard_map/ppermute | solution.py:325
  9.7 19.9 %collective-permute-start.19 = (f32[8,128,128]{2,1,0:T(8,128)}, f32[8,128,128]{2,1,0:T(8,128)}, u32[]{:S(2)}, u32[]{:S(2)}) collective-permute-start(f32[8,128,128]{2,1,0:T(8,128)} %get-tuple-element.73), channel_id=1, source_target_pairs={{0,8},{1,9},{2,10},{3,11},{4,12},{5,13},{6,14},{7,15},{8,0},{9,1},... | collective-permute-start | bytes 1572872 | tf_op jit(solution)/shard_map/ppermute | solution.py:325
  9.7 30.5 %collective-permute-start.3 = (f32[8,128,128]{2,1,0:T(8,128)}, f32[8,128,128]{2,1,0:T(8,128)S(1)}, u32[]{:S(2)}, u32[]{:S(2)}) collective-permute-start(f32[8,128,128]{2,1,0:T(8,128)} %get-tuple-element.76), channel_id=1, source_target_pairs={{0,24},{1,25},{2,26},{3,27},{4,28},{5,29},{6,30},{7,31},{8,16},{9,... | collective-permute-start | bytes 1572872 | tf_op jit(solution)/shard_map/ppermute | solution.py:325
  17.8 33.6 %collective-permute-start.4 = (f32[8,128,128]{2,1,0:T(8,128)S(1)}, f32[8,128,128]{2,1,0:T(8,128)S(1)}, u32[]{:S(2)}, u32[]{:S(2)}) collective-permute-start(f32[8,128,128]{2,1,0:T(8,128)S(1)} %get-tuple-element.75), channel_id=1, source_target_pairs={{0,16},{1,17},{2,18},{3,19},{4,20},{5,21},{6,22},{7,23},{8,24},{9,... | collective-permute-start | bytes 1572872 | tf_op jit(solution)/shard_map/ppermute | solution.py:325
  29.1 25.7 %collective-permute-start.5 = (f32[8,128,128]{2,1,0:T(8,128)S(1)}, f32[8,128,128]{2,1,0:T(8,128)}, u32[]{:S(2)}, u32[]{:S(2)}) collective-permute-start(f32[8,128,128]{2,1,0:T(8,128)S(1)} %get-tuple-element.74), channel_id=1, source_target_pairs={{0,8},{1,9},{2,10},{3,11},{4,12},{5,13},{6,14},{7,15},{8,0},{9,1},... | collective-permute-start | bytes 1572872 | tf_op jit(solution)/shard_map/ppermute | solution.py:325
  31.4 28.2 %collective-permute-start.20 = (f32[8,128,128]{2,1,0:T(8,128)S(1)}, f32[8,128,128]{2,1,0:T(8,128)S(1)}, u32[]{:S(2)}, u32[]{:S(2)}) collective-permute-start(f32[8,128,128]{2,1,0:T(8,128)S(1)} %get-tuple-element.64), channel_id=1, source_target_pairs={{0,6},{1,7},{2,0},{3,1},{4,2},{5,3},{6,4},{7,5},{8,14},{9,15},{10,... | collective-permute-start | bytes 1572872 | tf_op jit(solution)/shard_map/ppermute | solution.py:325
  40.3 36.3 %collective-permute-start.21 = (f32[8,128,128]{2,1,0:T(8,128)S(1)}, f32[8,128,128]{2,1,0:T(8,128)S(1)}, u32[]{:S(2)}, u32[]{:S(2)}) collective-permute-start(f32[8,128,128]{2,1,0:T(8,128)S(1)} %get-tuple-element.63), channel_id=1, source_target_pairs={{0,4},{1,5},{2,6},{3,7},{4,0},{5,1},{6,2},{7,3},{8,12},{9,13},{10,... | collective-permute-start | bytes 1572872 | tf_op jit(solution)/shard_map/ppermute | solution.py:325
  51.4 29.5 %collective-permute-start.22 = (f32[8,128,128]{2,1,0:T(8,128)S(1)}, f32[8,128,128]{2,1,0:T(8,128)S(1)}, u32[]{:S(2)}, u32[]{:S(2)}) collective-permute-start(f32[8,128,128]{2,1,0:T(8,128)S(1)} %get-tuple-element.62), channel_id=1, source_target_pairs={{0,2},{1,3},{2,4},{3,5},{4,6},{5,7},{6,0},{7,1},{8,10},{9,11},{10,... | collective-permute-start | bytes 1572872 | tf_op jit(solution)/shard_map/ppermute | solution.py:325
  52.7 92.7 %collective-permute-start.1 = (f32[16,128,128]{2,1,0:T(8,128)}, f32[16,128,128]{2,1,0:T(8,128)S(1)}, u32[]{:S(2)}, u32[]{:S(2)}) collective-permute-start(f32[16,128,128]{2,1,0:T(8,128)} %collective-permute-done.refs_0_), channel_id=1, source_target_pairs={{2,0},{3,1},{4,2},{5,3},{6,4},{7,5},{10,8},{11,9},{12,10},{13,11},... | collective-permute-start | bytes 3145736 | tf_op jit(solution)/shard_map/ppermute | solution.py:325
  54.8 90.6 %collective-permute-start.2 = (f32[16,128,128]{2,1,0:T(8,128)}, f32[16,128,128]{2,1,0:T(8,128)S(1)}, u32[]{:S(2)}, u32[]{:S(2)}) collective-permute-start(f32[16,128,128]{2,1,0:T(8,128)} %collective-permute-done.refs_0_), channel_id=1, source_target_pairs={{0,2},{1,3},{2,4},{3,5},{4,6},{5,7},{8,10},{9,11},{10,12},{11,13},... | collective-permute-start | bytes 3145736 | tf_op jit(solution)/shard_map/ppermute | solution.py:325
  59.6 77.5 %collective-permute-start.8 = (f32[8,128,128]{2,1,0:T(8,128)S(1)}, f32[8,128,128]{2,1,0:T(8,128)S(1)}, u32[]{:S(2)}, u32[]{:S(2)}) collective-permute-start(f32[8,128,128]{2,1,0:T(8,128)S(1)} %get-tuple-element.66), channel_id=1, source_target_pairs={{0,2},{1,3},{2,4},{3,5},{4,6},{5,7},{6,0},{7,1},{8,10},{9,11},{10,... | collective-permute-start | bytes 1572872 | tf_op jit(solution)/shard_map/ppermute | solution.py:325
  76.6 61.7 %collective-permute-start.6 = (f32[8,128,128]{2,1,0:T(8,128)S(1)}, f32[8,128,128]{2,1,0:T(8,128)S(1)}, u32[]{:S(2)}, u32[]{:S(2)}) collective-permute-start(f32[8,128,128]{2,1,0:T(8,128)S(1)} %get-tuple-element.68), channel_id=1, source_target_pairs={{0,6},{1,7},{2,0},{3,1},{4,2},{5,3},{6,4},{7,5},{8,14},{9,15},{10,... | collective-permute-start | bytes 1572872 | tf_op jit(solution)/shard_map/ppermute | solution.py:325
  80.9 63.1 %collective-permute-start.7 = (f32[8,128,128]{2,1,0:T(8,128)S(1)}, f32[8,128,128]{2,1,0:T(8,128)S(1)}, u32[]{:S(2)}, u32[]{:S(2)}) collective-permute-start(f32[8,128,128]{2,1,0:T(8,128)S(1)} %get-tuple-element.67), channel_id=1, source_target_pairs={{0,4},{1,5},{2,6},{3,7},{4,0},{5,1},{6,2},{7,3},{8,12},{9,13},{10,... | collective-permute-start | bytes 1572872 | tf_op jit(solution)/shard_map/ppermute | solution.py:325
  137.1 47.0 %collective-permute-start.23 = (f32[4,8,128,128]{3,2,1,0:T(8,128)}, f32[4,8,128,128]{3,2,1,0:T(8,128)}, u32[]{:S(2)}, u32[]{:S(2)}) collective-permute-start(f32[4,8,128,128]{3,2,1,0:T(8,128)} %pad_maximum_fusion.1.refs_8_), channel_id=1, source_target_pairs={{0,16},{1,17},{2,18},{3,19},{4,20},{5,21},{6,22},{7,23},{8,24},{9,... | collective-permute-start | bytes 6291464 | tf_op jit(solution)/shard_map/ppermute | solution.py:325
  145.4 38.6 %copy-start.4 = (f32[16,128,128]{2,1,0:T(8,128)}, f32[16,128,128]{2,1,0:T(8,128)S(1)}, u32[]{:S(2)}) copy-start(f32[16,128,128]{2,1,0:T(8,128)S(1)} %collective-permute-done.1) | copy-start | bytes 3145732
  145.4 38.6 %copy-start.6 = (f32[16,128,128]{2,1,0:T(8,128)}, f32[16,128,128]{2,1,0:T(8,128)S(1)}, u32[]{:S(2)}) copy-start(f32[16,128,128]{2,1,0:T(8,128)S(1)} %collective-permute-done.2) | copy-start | bytes 3145732
  145.5 27.5 %collective-permute-start.11 = (f32[16,128,128]{2,1,0:T(8,128)S(1)}, f32[16,128,128]{2,1,0:T(8,128)S(1)}, u32[]{:S(2)}, u32[]{:S(2)}) collective-permute-start(f32[16,128,128]{2,1,0:T(8,128)S(1)} %collective-permute-done.1), channel_id=1, source_target_pairs={{2,0},{3,1},{4,2},{5,3},{10,8},{11,9},{12,10},{13,11},{18,16},{19,... | collective-permute-start | bytes 3145736 | tf_op jit(solution)/shard_map/ppermute | solution.py:325
  151.1 26.0 %collective-permute-start.9 = (f32[16,128,128]{2,1,0:T(8,128)S(1)}, f32[16,128,128]{2,1,0:T(8,128)}, u32[]{:S(2)}, u32[]{:S(2)}) collective-permute-start(f32[16,128,128]{2,1,0:T(8,128)S(1)} %collective-permute-done.2), channel_id=1, source_target_pairs={{2,4},{3,5},{4,6},{5,7},{10,12},{11,13},{12,14},{13,15},{18,20},{1... | collective-permute-start | bytes 3145736 | tf_op jit(solution)/shard_map/ppermute | solution.py:325
  153.6 103.8 %collective-permute-start.25 = (f32[4,8,128,128]{3,2,1,0:T(8,128)}, f32[4,8,128,128]{3,2,1,0:T(8,128)}, u32[]{:S(2)}, u32[]{:S(2)}) collective-permute-start(f32[4,8,128,128]{3,2,1,0:T(8,128)} %pad_maximum_fusion.1.refs_8_), channel_id=1, source_target_pairs={{0,1},{1,0},{2,3},{3,2},{4,5},{5,4},{6,7},{7,6},{8,9},{9,8},{10,11... | collective-permute-start | bytes 6291464 | tf_op jit(solution)/shard_map/ppermute | solution.py:325
  155.0 103.0 %collective-permute-start.29 = (f32[4,8,128,128]{3,2,1,0:T(8,128)}, f32[4,8,128,128]{3,2,1,0:T(8,128)}, u32[]{:S(2)}, u32[]{:S(2)}) collective-permute-start(f32[4,8,128,128]{3,2,1,0:T(8,128)} %pad_maximum_fusion.refs_10_), channel_id=1, source_target_pairs={{0,1},{1,0},{2,3},{3,2},{4,5},{5,4},{6,7},{7,6},{8,9},{9,8},{10,11... | collective-permute-start | bytes 6291464 | tf_op jit(solution)/shard_map/ppermute | solution.py:325
  173.0 16.5 %collective-permute-start.12 = (f32[16,128,128]{2,1,0:T(8,128)S(1)}, f32[16,128,128]{2,1,0:T(8,128)S(1)}, u32[]{:S(2)}, u32[]{:S(2)}) collective-permute-start(f32[16,128,128]{2,1,0:T(8,128)S(1)} %collective-permute-done.11), channel_id=1, source_target_pairs={{2,0},{3,1},{10,8},{11,9},{18,16},{19,17},{26,24},{27,25}} | collective-permute-start | bytes 3145736 | tf_op jit(solution)/shard_map/ppermute | solution.py:325
  177.0 83.3 %collective-permute-start.27 = (f32[4,8,128,128]{3,2,1,0:T(8,128)}, f32[4,8,128,128]{3,2,1,0:T(8,128)}, u32[]{:S(2)}, u32[]{:S(2)}) collective-permute-start(f32[4,8,128,128]{3,2,1,0:T(8,128)} %pad_maximum_fusion.refs_10_), channel_id=1, source_target_pairs={{0,16},{1,17},{2,18},{3,19},{4,20},{5,21},{6,22},{7,23},{8,24},{9,... | collective-permute-start | bytes 6291464 | tf_op jit(solution)/shard_map/ppermute | solution.py:325
  184.1 73.4 %collective-permute-start.40 = (f32[16,128,128]{2,1,0:T(8,128)}, f32[16,128,128]{2,1,0:T(8,128)S(1)}, u32[]{:S(2)}, u32[]{:S(2)}) collective-permute-start(f32[16,128,128]{2,1,0:T(8,128)} %get-tuple-element.79), channel_id=1, source_target_pairs={{0,0},{1,8},{2,2},{3,10},{4,4},{5,12},{6,6},{7,14},{8,1},{9,9},{10... | collective-permute-start | bytes 3145736 | tf_op jit(solution)/shard_map/ppermute | solution.py:325
  190.5 68.9 %collective-permute-start.10 = (f32[16,128,128]{2,1,0:T(8,128)}, f32[16,128,128]{2,1,0:T(8,128)}, u32[]{:S(2)}, u32[]{:S(2)}) collective-permute-start(f32[16,128,128]{2,1,0:T(8,128)} %collective-permute-done.9), channel_id=1, source_target_pairs={{4,6},{5,7},{12,14},{13,15},{20,22},{21,23},{28,30},{29,31}} | collective-permute-start | bytes 3145736 | tf_op jit(solution)/shard_map/ppermute | solution.py:325
  197.0 63.2 %copy-start.5 = (f32[16,128,128]{2,1,0:T(8,128)S(1)}, f32[16,128,128]{2,1,0:T(8,128)}, u32[]{:S(2)}) copy-start(f32[16,128,128]{2,1,0:T(8,128)} %copy-done.4) | copy-start | bytes 3145732
  197.1 63.3 %copy-start.10 = (f32[16]{0:T(128)S(1)}, f32[16]{0:T(128)}, u32[]{:S(2)}) copy-start(f32[16]{0:T(128)} %param.5) | copy-start | bytes 196
  257.5 8.0 %collective-permute-start.13 = (f32[16,128,128]{2,1,0:T(8,128)}, f32[16,128,128]{2,1,0:T(8,128)}, u32[]{:S(2)}, u32[]{:S(2)}) collective-permute-start(f32[16,128,128]{2,1,0:T(8,128)} %collective-permute-done.refs_0_), channel_id=1, source_target_pairs={{0,8},{1,9},{2,10},{3,11},{4,12},{5,13},{6,14},{7,15},{8,0},{9,1},... | collective-permute-start | bytes 3145736 | tf_op jit(solution)/shard_map/ppermute | solution.py:325
  257.5 9.3 %collective-permute-start.15 = (f32[16,128,128]{2,1,0:T(8,128)S(1)}, f32[16,128,128]{2,1,0:T(8,128)}, u32[]{:S(2)}, u32[]{:S(2)}) collective-permute-start(f32[16,128,128]{2,1,0:T(8,128)S(1)} %broadcast_select_fusion.3.refs_2_), channel_id=1, source_target_pairs={{0,8},{1,9},{2,10},{3,11},{4,12},{5,13},{6,14},{7,15},{8,0},{9,1},... | collective-permute-start | bytes 3145736 | tf_op jit(solution)/shard_map/ppermute | solution.py:325
  258.0 24.9 %collective-permute-start.24 = (f32[2,8,128,128]{3,2,1,0:T(8,128)}, f32[2,8,128,128]{3,2,1,0:T(8,128)}, u32[]{:S(2)}, u32[]{:S(2)}) collective-permute-start(f32[2,8,128,128]{3,2,1,0:T(8,128)} %slice.152), channel_id=1, source_target_pairs={{0,1},{1,0},{2,3},{3,2},{4,5},{5,4},{6,7},{7,6},{8,9},{9,8},{10,11... | collective-permute-start | bytes 3145736 | tf_op jit(solution)/shard_map/ppermute | solution.py:325
  259.5 24.6 %collective-permute-start.16 = (f32[16,128,128]{2,1,0:T(8,128)S(1)}, f32[16,128,128]{2,1,0:T(8,128)}, u32[]{:S(2)}, u32[]{:S(2)}) collective-permute-start(f32[16,128,128]{2,1,0:T(8,128)S(1)} %broadcast_select_fusion.1.refs_3_), channel_id=1, source_target_pairs={{0,8},{1,9},{2,10},{3,11},{4,12},{5,13},{6,14},{7,15},{8,0},{9,1},... | collective-permute-start | bytes 3145736 | tf_op jit(solution)/shard_map/ppermute | solution.py:325
  260.3 25.7 %collective-permute-start.14 = (f32[16,128,128]{2,1,0:T(8,128)S(1)}, f32[16,128,128]{2,1,0:T(8,128)}, u32[]{:S(2)}, u32[]{:S(2)}) collective-permute-start(f32[16,128,128]{2,1,0:T(8,128)S(1)} %broadcast_select_fusion.5.refs_1_), channel_id=1, source_target_pairs={{0,8},{1,9},{2,10},{3,11},{4,12},{5,13},{6,14},{7,15},{8,0},{9,1},... | collective-permute-start | bytes 3145736 | tf_op jit(solution)/shard_map/ppermute | solution.py:325
  265.5 52.5 %collective-permute-start.26 = (f32[2,8,128,128]{3,2,1,0:T(8,128)S(1)}, f32[2,8,128,128]{3,2,1,0:T(8,128)S(1)}, u32[]{:S(2)}, u32[]{:S(2)}) collective-permute-start(f32[2,8,128,128]{3,2,1,0:T(8,128)S(1)} %slice.153), channel_id=1, source_target_pairs={{0,16},{1,17},{2,18},{3,19},{4,20},{5,21},{6,22},{7,23},{8,24},{9,... | collective-permute-start | bytes 3145736 | tf_op jit(solution)/shard_map/ppermute | solution.py:325
  266.7 51.3 %collective-permute-start.28 = (f32[2,8,128,128]{3,2,1,0:T(8,128)S(1)}, f32[2,8,128,128]{3,2,1,0:T(8,128)}, u32[]{:S(2)}, u32[]{:S(2)}) collective-permute-start(f32[2,8,128,128]{3,2,1,0:T(8,128)S(1)} %slice.154), channel_id=1, source_target_pairs={{0,1},{1,0},{2,3},{3,2},{4,5},{5,4},{6,7},{7,6},{8,9},{9,8},{10,11... | collective-permute-start | bytes 3145736 | tf_op jit(solution)/shard_map/ppermute | solution.py:325
  282.9 35.2 %collective-permute-start.30 = (f32[2,8,128,128]{3,2,1,0:T(8,128)S(1)}, f32[2,8,128,128]{3,2,1,0:T(8,128)}, u32[]{:S(2)}, u32[]{:S(2)}) collective-permute-start(f32[2,8,128,128]{3,2,1,0:T(8,128)S(1)} %slice.155), channel_id=1, source_target_pairs={{0,16},{1,17},{2,18},{3,19},{4,20},{5,21},{6,22},{7,23},{8,24},{9,... | collective-permute-start | bytes 3145736 | tf_op jit(solution)/shard_map/ppermute | solution.py:325
  284.1 28.3 %collective-permute-start.42 = (f32[16,128,128]{2,1,0:T(8,128)S(1)}, f32[16,128,128]{2,1,0:T(8,128)S(1)}, u32[]{:S(2)}, u32[]{:S(2)}) collective-permute-start(f32[16,128,128]{2,1,0:T(8,128)S(1)} %copy-done.1), channel_id=1, source_target_pairs={{0,2},{1,3},{2,4},{3,5},{4,6},{5,7},{8,10},{9,11},{10,12},{11,13},... | collective-permute-start | bytes 3145736 | tf_op jit(solution)/shard_map/ppermute | solution.py:325
  286.0 28.3 %collective-permute-start.41 = (f32[16,128,128]{2,1,0:T(8,128)S(1)}, f32[16,128,128]{2,1,0:T(8,128)S(1)}, u32[]{:S(2)}, u32[]{:S(2)}) collective-permute-start(f32[16,128,128]{2,1,0:T(8,128)S(1)} %copy-done.1), channel_id=1, source_target_pairs={{2,0},{3,1},{4,2},{5,3},{6,4},{7,5},{10,8},{11,9},{12,10},{13,11},... | collective-permute-start | bytes 3145736 | tf_op jit(solution)/shard_map/ppermute | solution.py:325
  312.4 32.2 %collective-permute-start.43 = (f32[16,128,128]{2,1,0:T(8,128)S(1)}, f32[16,128,128]{2,1,0:T(8,128)S(1)}, u32[]{:S(2)}, u32[]{:S(2)}) collective-permute-start(f32[16,128,128]{2,1,0:T(8,128)S(1)} %collective-permute-done.42), channel_id=1, source_target_pairs={{2,4},{3,5},{4,6},{5,7},{10,12},{11,13},{12,14},{13,15},{18,20},{1... | collective-permute-start | bytes 3145736 | tf_op jit(solution)/shard_map/ppermute | solution.py:325
  314.3 31.7 %collective-permute-start.45 = (f32[16,128,128]{2,1,0:T(8,128)S(1)}, f32[16,128,128]{2,1,0:T(8,128)S(1)}, u32[]{:S(2)}, u32[]{:S(2)}) collective-permute-start(f32[16,128,128]{2,1,0:T(8,128)S(1)} %collective-permute-done.41), channel_id=1, source_target_pairs={{2,0},{3,1},{4,2},{5,3},{10,8},{11,9},{12,10},{13,11},{18,16},{19,... | collective-permute-start | bytes 3145736 | tf_op jit(solution)/shard_map/ppermute | solution.py:325
  341.8 27.8 %collective-permute-start.31 = (f32[2,16,128,128]{3,2,1,0:T(8,128)}, f32[2,16,128,128]{3,2,1,0:T(8,128)S(1)}, u32[]{:S(2)}, u32[]{:S(2)}) collective-permute-start(f32[2,16,128,128]{3,2,1,0:T(8,128)} %get-tuple-element.32), channel_id=1, source_target_pairs={{0,8},{1,9},{2,10},{3,11},{4,12},{5,13},{6,14},{7,15},{8,0},{9,1},... | collective-permute-start | bytes 6291464 | tf_op jit(solution)/shard_map/ppermute | solution.py:325
  344.6 24.0 %collective-permute-start.44 = (f32[16,128,128]{2,1,0:T(8,128)S(1)}, f32[16,128,128]{2,1,0:T(8,128)S(1)}, u32[]{:S(2)}, u32[]{:S(2)}) collective-permute-start(f32[16,128,128]{2,1,0:T(8,128)S(1)} %collective-permute-done.43), channel_id=1, source_target_pairs={{4,6},{5,7},{12,14},{13,15},{20,22},{21,23},{28,30},{29,31}} | collective-permute-start | bytes 3145736 | tf_op jit(solution)/shard_map/ppermute | solution.py:325
  345.9 24.2 %collective-permute-start.32 = (f32[2,16,128,128]{3,2,1,0:T(8,128)}, f32[2,16,128,128]{3,2,1,0:T(8,128)S(1)}, u32[]{:S(2)}, u32[]{:S(2)}) collective-permute-start(f32[2,16,128,128]{3,2,1,0:T(8,128)} %get-tuple-element.34), channel_id=1, source_target_pairs={{0,8},{1,9},{2,10},{3,11},{4,12},{5,13},{6,14},{7,15},{8,0},{9,1},... | collective-permute-start | bytes 6291464 | tf_op jit(solution)/shard_map/ppermute | solution.py:325
  346.1 23.3 %collective-permute-start.46 = (f32[16,128,128]{2,1,0:T(8,128)S(1)}, f32[16,128,128]{2,1,0:T(8,128)S(1)}, u32[]{:S(2)}, u32[]{:S(2)}) collective-permute-start(f32[16,128,128]{2,1,0:T(8,128)S(1)} %collective-permute-done.45), channel_id=1, source_target_pairs={{2,0},{3,1},{10,8},{11,9},{18,16},{19,17},{26,24},{27,25}} | collective-permute-start | bytes 3145736 | tf_op jit(solution)/shard_map/ppermute | solution.py:325
  346.8 26.7 %collective-permute-start.47 = (f32[16,128,128]{2,1,0:T(8,128)S(1)}, f32[16,128,128]{2,1,0:T(8,128)S(1)}, u32[]{:S(2)}, u32[]{:S(2)}) collective-permute-start(f32[16,128,128]{2,1,0:T(8,128)S(1)} %copy-done.1), channel_id=1, source_target_pairs={{0,8},{1,9},{2,10},{3,11},{4,12},{5,13},{6,14},{7,15},{8,0},{9,1},... | collective-permute-start | bytes 3145736 | tf_op jit(solution)/shard_map/ppermute | solution.py:325
  368.6 5.8 %collective-permute-start.49 = (f32[16,128,128]{2,1,0:T(8,128)S(1)}, f32[16,128,128]{2,1,0:T(8,128)S(1)}, u32[]{:S(2)}, u32[]{:S(2)}) collective-permute-start(f32[16,128,128]{2,1,0:T(8,128)S(1)} %broadcast_select_fusion.2.refs_2_), channel_id=1, source_target_pairs={{0,8},{1,9},{2,10},{3,11},{4,12},{5,13},{6,14},{7,15},{8,0},{9,1},... | collective-permute-start | bytes 3145736 | tf_op jit(solution)/shard_map/ppermute | solution.py:325
  369.4 5.1 collective-permute-start.48
  369.6 4.9 collective-permute-start.50
  372.2 26.8 %collective-permute-start.33 = (f32[16,128,128]{2,1,0:T(8,128)S(1)}, f32[16,128,128]{2,1,0:T(8,128)S(1)}, u32[]{:S(2)}, u32[]{:S(2)}) collective-permute-start(f32[16,128,128]{2,1,0:T(8,128)S(1)} %get-tuple-element.38), channel_id=1, source_target_pairs={{6,4},{7,5},{14,12},{15,13},{22,20},{23,21},{30,28},{31,29}} | collective-permute-start | bytes 3145736 | tf_op jit(solution)/shard_map/ppermute | solution.py:325
  373.5 25.5 %collective-permute-start.34 = (f32[16,128,128]{2,1,0:T(8,128)S(1)}, f32[16,128,128]{2,1,0:T(8,128)S(1)}, u32[]{:S(2)}, u32[]{:S(2)}) collective-permute-start(f32[16,128,128]{2,1,0:T(8,128)S(1)} %get-tuple-element.39), channel_id=1, source_target_pairs={{0,2},{1,3},{8,10},{9,11},{16,18},{17,19},{24,26},{25,27}} | collective-permute-start | bytes 3145736 | tf_op jit(solution)/shard_map/ppermute | solution.py:325
  421.6 4.8 collective-permute-start.51
  422.4 7.0 %collective-permute-start.52 = (f32[2,16,128,128]{3,2,1,0:T(8,128)}, f32[2,16,128,128]{3,2,1,0:T(8,128)S(1)}, u32[]{:S(2)}, u32[]{:S(2)}) collective-permute-start(f32[2,16,128,128]{3,2,1,0:T(8,128)} %get-tuple-element.49), channel_id=1, source_target_pairs={{0,8},{1,9},{2,10},{3,11},{4,12},{5,13},{6,14},{7,15},{8,0},{9,1},... | collective-permute-start | bytes 6291464 | tf_op jit(solution)/shard_map/ppermute | solution.py:325
  432.3 26.2 %collective-permute-start.53 = (f32[16,128,128]{2,1,0:T(8,128)S(1)}, f32[16,128,128]{2,1,0:T(8,128)S(1)}, u32[]{:S(2)}, u32[]{:S(2)}) collective-permute-start(f32[16,128,128]{2,1,0:T(8,128)S(1)} %get-tuple-element.52), channel_id=1, source_target_pairs={{6,4},{7,5},{14,12},{15,13},{22,20},{23,21},{30,28},{31,29}} | collective-permute-start | bytes 3145736 | tf_op jit(solution)/shard_map/ppermute | solution.py:325
  433.6 24.9 %collective-permute-start.56 = (f32[16,128,128]{2,1,0:T(8,128)S(1)}, f32[16,128,128]{2,1,0:T(8,128)S(1)}, u32[]{:S(2)}, u32[]{:S(2)}) collective-permute-start(f32[16,128,128]{2,1,0:T(8,128)S(1)} %get-tuple-element.50), channel_id=1, source_target_pairs={{0,2},{1,3},{8,10},{9,11},{16,18},{17,19},{24,26},{25,27}} | collective-permute-start | bytes 3145736 | tf_op jit(solution)/shard_map/ppermute | solution.py:325
  434.4 46.7 %collective-permute-start.35 = (f32[16,128,128]{2,1,0:T(8,128)S(1)}, f32[16,128,128]{2,1,0:T(8,128)S(1)}, u32[]{:S(2)}, u32[]{:S(2)}) collective-permute-start(f32[16,128,128]{2,1,0:T(8,128)S(1)} %get-tuple-element.40), channel_id=1, source_target_pairs={{4,2},{5,3},{6,4},{7,5},{12,10},{13,11},{14,12},{15,13},{20,18},{2... | collective-permute-start | bytes 3145736 | tf_op jit(solution)/shard_map/ppermute | solution.py:325
  436.3 46.8 %collective-permute-start.37 = (f32[16,128,128]{2,1,0:T(8,128)S(1)}, f32[16,128,128]{2,1,0:T(8,128)S(1)}, u32[]{:S(2)}, u32[]{:S(2)}) collective-permute-start(f32[16,128,128]{2,1,0:T(8,128)S(1)} %get-tuple-element.41), channel_id=1, source_target_pairs={{0,2},{1,3},{2,4},{3,5},{8,10},{9,11},{10,12},{11,13},{16,18},{17,... | collective-permute-start | bytes 3145736 | tf_op jit(solution)/shard_map/ppermute | solution.py:325
  458.8 44.7 %collective-permute-start.54 = (f32[16,128,128]{2,1,0:T(8,128)S(1)}, f32[16,128,128]{2,1,0:T(8,128)S(1)}, u32[]{:S(2)}, u32[]{:S(2)}) collective-permute-start(f32[16,128,128]{2,1,0:T(8,128)S(1)} %get-tuple-element.81), channel_id=1, source_target_pairs={{4,2},{5,3},{6,4},{7,5},{12,10},{13,11},{14,12},{15,13},{20,18},{2... | collective-permute-start | bytes 3145736 | tf_op jit(solution)/shard_map/ppermute | solution.py:325
  460.7 44.8 %collective-permute-start.57 = (f32[16,128,128]{2,1,0:T(8,128)S(1)}, f32[16,128,128]{2,1,0:T(8,128)S(1)}, u32[]{:S(2)}, u32[]{:S(2)}) collective-permute-start(f32[16,128,128]{2,1,0:T(8,128)S(1)} %get-tuple-element.82), channel_id=1, source_target_pairs={{0,2},{1,3},{2,4},{3,5},{8,10},{9,11},{10,12},{11,13},{16,18},{17,... | collective-permute-start | bytes 3145736 | tf_op jit(solution)/shard_map/ppermute | solution.py:325
  481.2 44.8 %collective-permute-start.36 = (f32[16,128,128]{2,1,0:T(8,128)S(1)}, f32[16,128,128]{2,1,0:T(8,128)S(1)}, u32[]{:S(2)}, u32[]{:S(2)}) collective-permute-start(f32[16,128,128]{2,1,0:T(8,128)S(1)} %add.225), channel_id=1, source_target_pairs={{2,0},{3,1},{4,2},{5,3},{6,4},{7,5},{10,8},{11,9},{12,10},{13,11},... | collective-permute-start | bytes 3145736 | tf_op jit(solution)/shard_map/ppermute | solution.py:325
  483.2 42.8 %collective-permute-start.38 = (f32[16,128,128]{2,1,0:T(8,128)S(1)}, f32[16,128,128]{2,1,0:T(8,128)S(1)}, u32[]{:S(2)}, u32[]{:S(2)}) collective-permute-start(f32[16,128,128]{2,1,0:T(8,128)S(1)} %add.227), channel_id=1, source_target_pairs={{0,2},{1,3},{2,4},{3,5},{4,6},{5,7},{8,10},{9,11},{10,12},{11,13},... | collective-permute-start | bytes 3145736 | tf_op jit(solution)/shard_map/ppermute | solution.py:325
  503.6 44.8 %collective-permute-start.55 = (f32[16,128,128]{2,1,0:T(8,128)S(1)}, f32[16,128,128]{2,1,0:T(8,128)S(1)}, u32[]{:S(2)}, u32[]{:S(2)}) collective-permute-start(f32[16,128,128]{2,1,0:T(8,128)S(1)} %add.238), channel_id=1, source_target_pairs={{2,0},{3,1},{4,2},{5,3},{6,4},{7,5},{10,8},{11,9},{12,10},{13,11},... | collective-permute-start | bytes 3145736 | tf_op jit(solution)/shard_map/ppermute | solution.py:325
  505.7 42.8 %collective-permute-start.58 = (f32[16,128,128]{2,1,0:T(8,128)S(1)}, f32[16,128,128]{2,1,0:T(8,128)S(1)}, u32[]{:S(2)}, u32[]{:S(2)}) collective-permute-start(f32[16,128,128]{2,1,0:T(8,128)S(1)} %add.241), channel_id=1, source_target_pairs={{0,2},{1,3},{2,4},{3,5},{4,6},{5,7},{8,10},{9,11},{10,12},{11,13},... | collective-permute-start | bytes 3145736 | tf_op jit(solution)/shard_map/ppermute | solution.py:325
  526.2 27.2 %collective-permute-start.39 = (f32[16,128,128]{2,1,0:T(8,128)S(1)}, f32[16,128,128]{2,1,0:T(8,128)S(1)}, u32[]{:S(2)}, u32[]{:S(2)}) collective-permute-start(f32[16,128,128]{2,1,0:T(8,128)S(1)} %add_add_fusion.1), channel_id=1, source_target_pairs={{0,0},{1,8},{2,2},{3,10},{4,4},{5,12},{6,6},{7,14},{8,1},{9,9},{10... | collective-permute-start | bytes 3145736 | tf_op jit(solution)/shard_map/ppermute | solution.py:325
  548.6 17.2 %collective-permute-start.59 = (f32[16,128,128]{2,1,0:T(8,128)S(1)}, f32[16,128,128]{2,1,0:T(8,128)S(1)}, u32[]{:S(2)}, u32[]{:S(2)}) collective-permute-start(f32[16,128,128]{2,1,0:T(8,128)S(1)} %add_add_fusion), channel_id=1, source_target_pairs={{0,0},{1,8},{2,2},{3,10},{4,4},{5,12},{6,6},{7,14},{8,1},{9,9},{10... | collective-permute-start | bytes 3145736 | tf_op jit(solution)/shard_map/ppermute | solution.py:325
  (11 other events, 39.6 us)
